TPU v7x, 32 devices: a whole 2x2x4 slice. The times are simulated.
32 devices in a mesh: rows: 16 (over z, y, x), cols: 2 (over core).
Axes of the slice: x: 2, y: 2, z: 4, core: 2. Of those that a mesh axis runs over, the one named last changes fastest.
Arguments:
- tokens_in: bfloat16 [6304, 768], P(('rows', 'cols')), may hold values from -6 to 6
- ln1_gain: float32 [768], replicated, may hold values from 0.5 to 1.5
- ln1_shift: float32 [768], replicated, may hold values from -4 to 4
- qkv_weight: bfloat16 [768, 2304], P(None, 'cols'), may hold values from -0.21875 to 0.21875
- out_weight: bfloat16 [768, 768], P('cols'), may hold values from -1.75 to 1.75
- ln2_gain: float32 [768], replicated, may hold values from 0.5 to 1.5
- ln2_shift: float32 [768], replicated, may hold values from -4 to 4
- router_weight: bfloat16 [768, 32], replicated, may hold values from -0.4375 to 0.4375
- expert_in: bfloat16 [768, 98304], P(None, ('rows', 'cols')), may hold values from -0.21875 to 0.21875
- expert_out: bfloat16 [98304, 768], P(('rows', 'cols')), may hold values from -0.4375 to 0.4375
- routes: int32 [6304, 2], P(('rows', 'cols')), may hold values from 0 to 31, all different within a row; in each aligned block of 197 rows (0 to 196, 197 to 393, ...) at most 16 rows name the same one
- cotangent: bfloat16 [6304, 768], P(('rows', 'cols')), may hold values from -6 to 6
Outputs:
- output: bfloat16 [6304, 768], P(('rows', 'cols'))
- tokens_grad: bfloat16 [6304, 768], P(('rows', 'cols'))
- ln1_gain_grad: float32 [768], replicated
- ln1_shift_grad: float32 [768], replicated
- qkv_grad: float32 [768, 2304], P(None, 'cols')
- out_grad: float32 [768, 768], P('cols')
- ln2_gain_grad: float32 [768], replicated
- ln2_shift_grad: float32 [768], replicated
- router_grad: float32 [768, 32], replicated
- expert_in_grad: float32 [768, 98304], P(None, ('rows', 'cols'))
- expert_out_grad: float32 [98304, 768], P(('rows', 'cols'))
Inputs may be any that keep to these rules, and one draw needn't show every extreme that they name: `routes`: the two experts of a token differ. Among the tokens of one device (aligned blocks of 197 rows) each expert is named by at most 16 assignments, a bound that some block reaches.
All inputs are finite; a program needn't handle non-finite values.
Results may differ from a plain program's by a relative error of at most 0.022.
Values may be sent and summed in bfloat16 or wider, within the bound.
A program may use at most 192 MiB of HBM per device.

v0:
```python
import jax
import jax.numpy as jnp
from jax import lax
from jax.sharding import PartitionSpec as P

DH = 64
FF = 3072
SEQ = 197


EPSILON = 1e-06


def layer_norm(values, norm_gain, norm_shift):
    average = jnp.mean(values, axis=-1, keepdims=True)
    centred = values - average
    variance = jnp.mean(centred * centred, axis=-1, keepdims=True)
    return centred * lax.rsqrt(variance + EPSILON) * norm_gain + norm_shift


def gelu_slope(pre_act):
    normal_cdf = 0.5 * (1.0 + jax.scipy.special.erf(pre_act * 0.7071067811865476))
    density = jnp.exp(-0.5 * pre_act * pre_act) * 0.3989422804014327
    return normal_cdf + pre_act * density


def dot_rows(first_side, second_side):
    return lax.dot_general(
        first_side, second_side, (((0,), (0,)), ((), ())), preferred_element_type=jnp.float32
    )


def dot_last(first_side, second_side):
    return lax.dot_general(
        first_side, second_side, (((1,), (1,)), ((), ())), preferred_element_type=jnp.float32
    )


def attention_scores(queries, keys_all, score_scale):
    scores = jnp.einsum("nqhd,nkhd->nhqk", queries, keys_all, preferred_element_type=jnp.float32)
    return scores * score_scale


def body(
    tokens_in,
    ln1_gain,
    ln1_shift,
    qkv_weight,
    out_weight,
    ln2_gain,
    ln2_shift,
    router_weight,
    expert_in,
    expert_out,
    routes,
    cotangent,
):
    local_rows = tokens_in.shape[0]
    model_width = tokens_in.shape[1]
    experts = router_weight.shape[1]
    capacity = max(2, 8 * local_rows // (3 * experts))
    heads_local = qkv_weight.shape[1] // (3 * DH)
    score_scale = DH ** (-0.5)
    row_count = lax.axis_size("rows")
    row_place = lax.axis_index("rows")
    col_place = lax.axis_index("cols")
    per_device = max(1, experts // row_count)
    copies = max(1, row_count // experts)
    slots = per_device * capacity
    piece_half = expert_in.shape[1]
    piece_whole = piece_half * lax.axis_size("cols")
    arrived_rows = row_count * slots
    tokens_f = tokens_in.astype(jnp.float32)
    normed_low = layer_norm(tokens_f, ln1_gain, ln1_shift).astype(jnp.bfloat16)
    gathered = lax.all_gather(normed_low, "cols", axis=0, tiled=True)
    pair_rows = gathered.shape[0]
    images = pair_rows // SEQ
    qkv_low = jnp.dot(gathered, qkv_weight, preferred_element_type=jnp.float32).astype(jnp.bfloat16)
    head_split = qkv_low.reshape(images, SEQ, heads_local, 3, DH)
    queries = head_split[:, :, :, 0]
    keys_all = head_split[:, :, :, 1]
    values_all = head_split[:, :, :, 2]
    scores = attention_scores(queries, keys_all, score_scale)
    score_peak = jnp.max(scores, axis=-1, keepdims=True)
    log_total = score_peak + jnp.log(jnp.sum(jnp.exp(scores - score_peak), axis=-1, keepdims=True))
    weights_low = jnp.exp(scores - log_total).astype(jnp.bfloat16)
    context = jnp.einsum(
        "nhqk,nkhd->nqhd", weights_low, values_all, preferred_element_type=jnp.float32
    )
    context_low = context.astype(jnp.bfloat16).reshape(pair_rows, heads_local * DH)
    row_block = context_low
    attn_out = lax.psum_scatter(
        jnp.dot(row_block, out_weight, preferred_element_type=jnp.float32),
        "cols",
        scatter_dimension=0,
        tiled=True,
    )
    hidden_one = tokens_f + attn_out
    mixed_low = layer_norm(hidden_one, ln2_gain, ln2_shift).astype(jnp.bfloat16)
    logits = jnp.dot(mixed_low, router_weight, preferred_element_type=jnp.float32)
    router_probs = jax.nn.softmax(logits, axis=-1)
    expert_ids = jnp.arange(experts, dtype=jnp.int32)
    chosen = (routes[:, :, None] == expert_ids[None, None, :]).astype(jnp.float32)
    gate_values = jnp.sum(router_probs[:, None, :] * chosen, axis=-1)
    flat_ids = routes.reshape(-1)
    flat_hot = (flat_ids[:, None] == expert_ids[None, :]).astype(jnp.int32)
    slot_ranks = jnp.sum(jnp.cumsum(flat_hot, axis=0) * flat_hot, axis=1) - 1
    first_device = flat_ids // per_device * copies
    slot_index = flat_ids % per_device * capacity + slot_ranks
    copy_ids = jnp.arange(copies, dtype=jnp.int32)
    targets = ((first_device[:, None] + copy_ids[None, :]) * slots + slot_index[:, None]).reshape(
        -1
    )
    grad_out = cotangent.astype(jnp.float32)
    grad_slots = (
        (gate_values[:, :, None] * grad_out[:, None, :])
        .astype(jnp.bfloat16)
        .reshape(2 * local_rows, model_width)
    )
    rows_send = (
        jnp.zeros((arrived_rows, model_width), jnp.bfloat16)
        .at[targets]
        .set(jnp.repeat(mixed_low, 2 * copies, axis=0))
    )
    grads_send = (
        jnp.zeros((arrived_rows, model_width), jnp.bfloat16)
        .at[targets]
        .set(jnp.repeat(grad_slots, copies, axis=0))
    )
    arrived, grad_result = (
        lax.all_to_all(
            rows_send.reshape(row_count, slots, model_width),
            "rows",
            split_axis=0,
            concat_axis=0,
            tiled=True,
        ),
        lax.all_to_all(
            grads_send.reshape(row_count, slots, model_width),
            "rows",
            split_axis=0,
            concat_axis=0,
            tiled=True,
        ),
    )
    arrived = arrived.reshape(arrived_rows, model_width)
    grad_result = grad_result.reshape(arrived_rows, model_width)
    unit_base = row_place % copies * piece_whole
    both_rows, both_grads = (
        lax.all_gather(arrived, "cols", axis=0, tiled=True),
        lax.all_gather(grad_result, "cols", axis=0, tiled=True),
    )
    slot_local = jnp.arange(both_rows.shape[0], dtype=jnp.int32) % slots // capacity
    unit_local = (
        unit_base + col_place * piece_half + jnp.arange(piece_half, dtype=jnp.int32)
    ) // FF
    mask = (slot_local[:, None] == unit_local[None, :]).astype(jnp.float32)
    pre_act = jnp.dot(both_rows, expert_in, preferred_element_type=jnp.float32) * mask
    act_low = jax.nn.gelu(pre_act, approximate=False).astype(jnp.bfloat16)
    result_low = lax.psum_scatter(
        jnp.dot(act_low, expert_out, preferred_element_type=jnp.float32).astype(jnp.bfloat16),
        "cols",
        scatter_dimension=0,
        tiled=True,
    )
    grad_act = dot_last(both_grads, expert_out)
    grad_pre_low = (grad_act * gelu_slope(pre_act) * mask).astype(jnp.bfloat16)
    first_grad = dot_rows(both_rows, grad_pre_low)
    second_grad = dot_rows(act_low, both_grads)
    grad_arrived = lax.psum_scatter(
        dot_last(grad_pre_low, expert_in).astype(jnp.bfloat16),
        "cols",
        scatter_dimension=0,
        tiled=True,
    )
    returned = lax.all_to_all(
        result_low.reshape(row_count, slots, model_width),
        "rows",
        split_axis=0,
        concat_axis=0,
        tiled=True,
    )
    returned = returned.reshape(arrived_rows, model_width)
    picked = jnp.sum(
        returned[targets].reshape(local_rows, 2, copies, model_width).astype(jnp.float32), axis=2
    )
    output = (hidden_one + jnp.sum(gate_values[:, :, None] * picked, axis=1)).astype(jnp.bfloat16)
    grad_gates = jnp.sum(grad_out[:, None, :] * picked, axis=-1)
    grad_sent = lax.all_to_all(
        grad_arrived.reshape(row_count, slots, model_width),
        "rows",
        split_axis=0,
        concat_axis=0,
        tiled=True,
    )
    grad_sent = grad_sent.reshape(arrived_rows, model_width)
    grad_mixed_experts = jnp.sum(
        grad_sent[targets].reshape(local_rows, 2 * copies, model_width).astype(jnp.float32), axis=1
    )
    gate_term = jnp.sum(grad_gates * gate_values, axis=-1, keepdims=True)
    grad_probs = jnp.sum(chosen * grad_gates[:, :, None], axis=1)
    grad_logits_low = (router_probs * (grad_probs - gate_term)).astype(jnp.bfloat16)
    router_grad = dot_rows(mixed_low, grad_logits_low)
    grad_mixed = dot_last(grad_logits_low, router_weight) + grad_mixed_experts
    unused_two, norm_two_back = jax.vjp(layer_norm, hidden_one, ln2_gain, ln2_shift)
    grad_hidden_part, ln2_gain_grad, ln2_shift_grad = norm_two_back(grad_mixed)
    grad_hidden = grad_out + grad_hidden_part
    grad_attn_low = grad_hidden.astype(jnp.bfloat16)
    grad_attn_all = lax.all_gather(grad_attn_low, "cols", axis=0, tiled=True)
    out_grad = dot_rows(context_low, grad_attn_all)
    grad_context = (
        dot_last(grad_attn_all, out_weight)
        .astype(jnp.bfloat16)
        .reshape(images, SEQ, heads_local, DH)
    )
    scores_again = attention_scores(queries, keys_all, score_scale)
    attn_probs = jnp.exp(scores_again - log_total)
    probs_low = attn_probs.astype(jnp.bfloat16)
    grad_values = jnp.einsum(
        "nhqk,nqhd->nkhd", probs_low, grad_context, preferred_element_type=jnp.float32
    )
    grad_weights = jnp.einsum(
        "nqhd,nkhd->nhqk", grad_context, values_all, preferred_element_type=jnp.float32
    )
    row_term = jnp.sum(grad_weights * attn_probs, axis=-1, keepdims=True)
    grad_scores = (attn_probs * (grad_weights - row_term)).astype(jnp.bfloat16)
    grad_queries = (
        jnp.einsum("nhqk,nkhd->nqhd", grad_scores, keys_all, preferred_element_type=jnp.float32)
        * score_scale
    )
    grad_keys = (
        jnp.einsum("nhqk,nqhd->nkhd", grad_scores, queries, preferred_element_type=jnp.float32)
        * score_scale
    )
    grad_qkv = (
        jnp.stack([grad_queries, grad_keys, grad_values], axis=3)
        .astype(jnp.bfloat16)
        .reshape(pair_rows, 3 * heads_local * DH)
    )
    qkv_grad = dot_rows(gathered, grad_qkv)
    row_block = grad_qkv
    grad_normed = lax.psum_scatter(
        dot_last(row_block, qkv_weight).astype(jnp.bfloat16),
        "cols",
        scatter_dimension=0,
        tiled=True,
    ).astype(jnp.float32)
    unused_one, norm_one_back = jax.vjp(layer_norm, tokens_f, ln1_gain, ln1_shift)
    grad_tokens_part, ln1_gain_grad, ln1_shift_grad = norm_one_back(grad_normed)
    tokens_grad = (grad_hidden + grad_tokens_part).astype(jnp.bfloat16)
    qkv_grad, out_grad = lax.psum((qkv_grad, out_grad), "rows")
    router_grad, ln1_gain_grad, ln1_shift_grad, ln2_gain_grad, ln2_shift_grad = lax.psum(
        (router_grad, ln1_gain_grad, ln1_shift_grad, ln2_gain_grad, ln2_shift_grad),
        ("rows", "cols"),
    )
    return (
        output,
        tokens_grad,
        ln1_gain_grad,
        ln1_shift_grad,
        qkv_grad,
        out_grad,
        ln2_gain_grad,
        ln2_shift_grad,
        router_grad,
        first_grad,
        second_grad,
    )


def solution(mesh):
    in_specs = (
        P(("rows", "cols"), None),
        P(),
        P(),
        P(None, "cols"),
        P("cols", None),
        P(),
        P(),
        P(),
        P(None, ("rows", "cols")),
        P(("rows", "cols"), None),
        P(("rows", "cols"), None),
        P(("rows", "cols"), None),
    )
    out_specs = (
        P(("rows", "cols"), None),
        P(("rows", "cols"), None),
        P(),
        P(),
        P(None, "cols"),
        P("cols", None),
        P(),
        P(),
        P(),
        P(None, ("rows", "cols")),
        P(("rows", "cols"), None),
    )
    return jax.shard_map(body, mesh=mesh, in_specs=in_specs, out_specs=out_specs, check_vma=False)
```

profile of v0, /device:TPU:0, one launch (start us, length us, event | category | flops | bytes accessed | tf_op | source)
XLA Modules:
  0.0 595.0 jit_solution(453533763309978735)
XLA Ops:
  14.9 2.8 reshape.405
  17.7 7.0 %fusion.72 = (bf16[2,197,6,1,64]{4,3,2,1,0:T(2,128)(2,1)S(1)}, bf16[2,197,6,1,64]{4,3,2,1,0:T(2,128)(2,1)}, bf16[2,197,6,1,64]{4,3,2,1,0:T(2,128)(2,1)}) fusion(bf16[2,197,6,3,64]{4,3,2,1,0:T(4,128)(2,1)} %reshape.405), kind=kLoop, calls=%fused_computation.161 | loop fusion | bytes 1815552 | tf_op jit(solution)/shard_map/slice | solution.py:80
  27.2 3.7 copy.122
  39.8 4.9 fusion
  56.2 3.9 scatter_custom_fusion
  60.0 8.3 %all-to-all-start = ((bf16[16,32,768]{2,1,0:T(8,128)(2,1)}), bf16[16,32,768]{2,1,0:T(8,128)(2,1)}, u32[]{:S(2)}, u32[]{:S(2)}) async-start(bf16[16,32,768]{2,1,0:T(8,128)(2,1)} %bitcast.8), calls=%async_computation | async-start | bytes 1572864 | tf_op jit(solution)/shard_map/all_to_all | solution.py:131
  72.2 15.5 %all-to-all-done = bf16[16,32,768]{2,1,0:T(8,128)(2,1)} async-done(((bf16[16,32,768]{2,1,0:T(8,128)(2,1)}), bf16[16,32,768]{2,1,0:T(8,128)(2,1)}, u32[]{:S(2)}, u32[]{:S(2)}) %all-to-all-start) | async-done | bytes 786464 | tf_op jit(solution)/shard_map/all_to_all | solution.py:131
  88.0 3.2 scatter_custom_fusion.1
  91.2 4.9 all-to-all-start.2
  96.2 18.6 %all-to-all-done.2 = bf16[16,32,768]{2,1,0:T(8,128)(2,1)S(1)} async-done(((bf16[16,32,768]{2,1,0:T(8,128)(2,1)}), bf16[16,32,768]{2,1,0:T(8,128)(2,1)S(1)}, u32[]{:S(2)}, u32[]{:S(2)}) %all-to-all-start.2) | async-done | bytes 786464 | tf_op jit(solution)/shard_map/all_to_all | solution.py:138
  115.8 35.3 %fusion.5 = (bf16[1024,3072]{1,0:T(8,128)(2,1)S(1)}, f32[1024,3072]{1,0:T(8,128)}) fusion(s32[3072]{0:T(1024)S(1)} %add_select_fusion, s32[1024]{0:T(1024)S(1)} %add_select_fusion.1, bf16[1024,768]{1,0:T(8,128)(2,1)} %all-gather.5.cloned.1.call-done, bf16[768,3072]{1,0:T(8,128)(2,1)} %param.20), kind=kOutput, calls=%fused_computation.11 | convolution fusion | flops 5042601984 | bytes 25182208 | tf_op jit(solution)/shard_map/dot_general | solution.py:158
  153.8 8.5 %convolution_convert_fusion.2 = bf16[1024,768]{1,0:T(8,128)(2,1)} fusion(bf16[1024,3072]{1,0:T(8,128)(2,1)S(1)} %get-tuple-element.37, bf16[3072,768]{1,0:T(8,128)(2,1)} %param.21), kind=kOutput, calls=%fused_computation.39 | convolution fusion | flops 4832624640 | bytes 12582912 | tf_op jit(solution)/shard_map/dot_general | solution.py:161
  162.3 8.7 %reduce-scatter.9.cloned.1.call-start = ((), (), s32[]{:S(2)}) async-start(), calls=%async_computation.9 | async-start | bytes 2359296 | tf_op jit(solution)/shard_map/reduce_scatter | solution.py:170
  171.1 12.0 %fusion.2 = bf16[1024,3072]{1,0:T(8,128)(2,1)S(1)} fusion(f32[1024,3072]{1,0:T(8,128)} %get-tuple-element.38, bf16[1024,768]{1,0:T(8,128)(2,1)} %all-gather.7.cloned.1.call-done, bf16[3072,768]{1,0:T(8,128)(2,1)} %param.21, s32[3072]{0:T(1024)S(1)} %add_select_fusion, s32[1024]{0:T(1024)S(1)} %add_select_fusion.1), kind=kOutput, calls=%fused_computation.8 | convolution fusion | flops 4872732672 | bytes 25182208 | tf_op jit(solution)/shard_map/dot_general | solution.py:34
  185.8 6.3 %convolution_convert_fusion.1 = bf16[1024,768]{1,0:T(8,128)(2,1)} fusion(bf16[1024,3072]{1,0:T(8,128)(2,1)S(1)} %fusion.2, bf16[768,3072]{1,0:T(8,128)(2,1)S(1)} %bitcast.115), kind=kOutput, calls=%fused_computation.38 | convolution fusion | flops 4832624640 | bytes 12582912 | tf_op jit(solution)/shard_map/dot_general | solution.py:34
  192.1 5.2 all-to-all-start.1
  197.2 3.5 reduce-scatter.9.cloned.1.call-done
  200.8 15.2 %all-to-all-done.1 = bf16[16,32,768]{2,1,0:T(8,128)(2,1)S(1)} async-done(((bf16[16,32,768]{2,1,0:T(8,128)(2,1)}), bf16[16,32,768]{2,1,0:T(8,128)(2,1)S(1)}, u32[]{:S(2)}, u32[]{:S(2)}) %all-to-all-start.1) | async-done | bytes 786464 | tf_op jit(solution)/shard_map/all_to_all | solution.py:176
  216.0 4.9 all-to-all-start.3
  225.4 2.8 reshape.365
  228.2 4.7 multiply_reduce_fusion.2
  234.1 5.3 all-to-all-done.3
  242.1 2.8 reshape.366
  260.9 3.2 fusion.22
  270.2 4.6 fusion.75
  276.4 10.0 %fusion.79 = f32[3072,768]{1,0:T(8,128)} fusion(bf16[1024,3072]{1,0:T(8,128)(2,1)} %copy-done.44, bf16[1024,768]{1,0:T(8,128)(2,1)} %all-gather.7.cloned.1.call-done), kind=kOutput, calls=%fused_computation.168 | convolution fusion | flops 4831838208 | bytes 17301504 | tf_op jit(solution)/shard_map/dot_general | solution.py:28
  287.7 3.4 fusion.1
  294.5 9.9 %fusion.78 = f32[768,3072]{1,0:T(8,128)} fusion(bf16[1024,768]{1,0:T(8,128)(2,1)} %all-gather.5.cloned.1.call-done, bf16[1024,3072]{1,0:T(8,128)(2,1)} %copy-done.43), kind=kOutput, calls=%fused_computation.167 | convolution fusion | flops 4831838208 | bytes 17301504 | tf_op jit(solution)/shard_map/dot_general | solution.py:28
  307.3 40.2 %all-reduce.5 = (f32[768]{0:T(1024)}, f32[768]{0:T(1024)}, f32[768]{0:T(1024)}, f32[768]{0:T(1024)}) all-reduce(f32[768]{0:T(1024)S(1)} %get-tuple-element.15, f32[768]{0:T(1024)S(1)} %get-tuple-element.18, f32[768]{0:T(1024)S(1)} %get-tuple-element.11, ...), channel_id=1, replica_groups=mesh['rows'=16,'cols'=2] {'rows','cols'}, use_global_device_ids=true, to_apply=%region_29.30 | all-reduce | flops 3072 | bytes 24576 | tf_op jit(solution)/shard_map/psum | solution.py:252
  348.6 46.3 %all-reduce.10.cloned.1.call-done = f32[768,32]{0,1:T(8,128)} async-done(((f32[768,32]{0,1:T(8,128)}), f32[768,32]{0,1:T(8,128)}) %all-reduce.10.cloned.1.call-update) | async-done | bytes 98320 | tf_op jit(solution)/shard_map/psum | solution.py:252
  394.8 187.2 %all-reduce.12.cloned.1.call-done = (f32[768,1152]{1,0:T(8,128)}, f32[384,768]{1,0:T(8,128)}) async-done(((f32[768,1152]{1,0:T(8,128)}, f32[384,768]{1,0:T(8,128)}), (f32[768,1152]{1,0:T(8,128)}, f32[384,768]{1,0:T(8,128)})) %all-reduce.12.cloned.1.call-update) | async-done | bytes 4718608 | tf_op jit(solution)/shard_map/psum | solution.py:251
  582.0 4.1 copy.130
  (201 shorter events, 82.3 us)
Async XLA Ops:
  35.1 12.4 %copy-start.31 = (s32[197,2]{0,1:T(2,128)S(1)}, s32[197,2]{0,1:T(2,128)}, u32[]{:S(2)}) copy-start(s32[197,2]{0,1:T(2,128)} %param.22) | copy-start | bytes 4732
  36.0 13.5 %copy-start.42 = (u32[32]{0:T(128)S(1)}, u32[32]{0:T(128)}, u32[]{:S(2)}) copy-start(u32[32]{0:T(128)} %constant.193) | copy-start | bytes 388
  36.0 16.9 %copy-start.5 = (bf16[197,768]{1,0:T(8,128)(2,1)S(1)}, bf16[197,768]{1,0:T(8,128)(2,1)}, u32[]{:S(2)}) copy-start(bf16[197,768]{1,0:T(8,128)(2,1)} %param.12) | copy-start | bytes 907780
  37.1 16.9 %copy-start.28 = (f32[768]{0:T(1024)S(1)}, f32[768]{0:T(1024)}, u32[]{:S(2)}) copy-start(f32[768]{0:T(1024)} %param.17) | copy-start | bytes 9220
  37.1 16.9 %copy-start.41 = (f32[768]{0:T(1024)S(1)}, f32[768]{0:T(1024)}, u32[]{:S(2)}) copy-start(f32[768]{0:T(1024)} %param.18) | copy-start | bytes 9220
  45.4 5.4 collective-permute-start
  47.9 20.5 %copy-start.9 = (bf16[197,768]{1,0:T(8,128)(2,1)S(1)}, bf16[197,768]{1,0:T(8,128)(2,1)}, u32[]{:S(2)}) copy-start(bf16[197,768]{1,0:T(8,128)(2,1)} %param.23) | copy-start | bytes 907780
  53.4 18.8 %copy-start.39 = (f32[197]{0:T(256)}, f32[197]{0:T(256)S(1)}, u32[]{:S(2)}) copy-start(f32[197]{0:T(256)S(1)} %multiply_reduce_fusion.6) | copy-start | bytes 2368
  53.4 18.5 %copy-start.25 = (bf16[768,32]{0,1:T(8,128)(2,1)S(1)}, bf16[768,32]{0,1:T(8,128)(2,1)}, u32[]{:S(2)}) copy-start(bf16[768,32]{0,1:T(8,128)(2,1)} %param.19) | copy-start | bytes 147460
  53.9 18.2 %copy-start.34 = (f32[197]{0:T(256)}, f32[197]{0:T(256)S(1)}, u32[]{:S(2)}) copy-start(f32[197]{0:T(256)S(1)} %fusion.67) | copy-start | bytes 2368
  54.1 33.6 %copy-start.11 = (bf16[197,768]{1,0:T(8,128)(2,1)}, bf16[197,768]{1,0:T(8,128)(2,1)S(1)}, u32[]{:S(2)}) copy-start(bf16[197,768]{1,0:T(8,128)(2,1)S(1)} %add_convert_fusion.2) | copy-start | bytes 907780
  60.0 27.7 %all-to-all-start = ((bf16[16,32,768]{2,1,0:T(8,128)(2,1)}), bf16[16,32,768]{2,1,0:T(8,128)(2,1)}, u32[]{:S(2)}, u32[]{:S(2)}) async-start(bf16[16,32,768]{2,1,0:T(8,128)(2,1)} %bitcast.8), calls=%async_computation | async-start | bytes 1572864 | tf_op jit(solution)/shard_map/all_to_all | solution.py:131
  68.3 47.4 %all-gather.5.cloned.1.call-start = ((), (), s32[]{:S(2)}) async-start(), calls=%async_computation.6 | async-start | bytes 2359296 | tf_op jit(solution)/shard_map/all_gather | solution.py:150
  72.2 15.5 %copy-start.36 = (f32[197]{0:T(256)}, f32[197]{0:T(256)S(1)}, u32[]{:S(2)}) copy-start(f32[197]{0:T(256)S(1)} %fusion.55) | copy-start | bytes 2368
  91.2 23.5 %all-to-all-start.2 = ((bf16[16,32,768]{2,1,0:T(8,128)(2,1)}), bf16[16,32,768]{2,1,0:T(8,128)(2,1)S(1)}, u32[]{:S(2)}, u32[]{:S(2)}) async-start(bf16[16,32,768]{2,1,0:T(8,128)(2,1)} %bitcast.107), calls=%async_computation.3 | async-start | bytes 1572864 | tf_op jit(solution)/shard_map/all_to_all | solution.py:138
  96.1 74.9 %all-gather.7.cloned.1.call-start = ((), (), s32[]{:S(2)}) async-start(), calls=%async_computation.8 | async-start | bytes 2359296 | tf_op jit(solution)/shard_map/all_gather | solution.py:151
  115.7 76.4 %reduce-scatter.7.cloned.1.call-start = ((), (), s32[]{:S(2)}) async-start(), calls=%async_computation.7 | async-start | bytes 2359296 | tf_op jit(solution)/shard_map/reduce_scatter | solution.py:160
  153.8 32.0 %slice-start = ((s8[4718592]{0:T(1024)(128)(4,1)}), s8[524288]{0:T(1024)(128)(4,1)S(1)}, s32[]{:S(2)}) async-start(s8[4718592]{0:T(1024)(128)(4,1)} %bitcast.114), calls=%async_computation.12 | async-start | bytes 1048576
  162.3 38.5 %reduce-scatter.9.cloned.1.call-start = ((), (), s32[]{:S(2)}) async-start(), calls=%async_computation.9 | async-start | bytes 2359296 | tf_op jit(solution)/shard_map/reduce_scatter | solution.py:170
  171.1 14.7 %slice-start.1 = ((s8[4718592]{0:T(1024)(128)(4,1)}), s8[4194304]{0:T(1024)(128)(4,1)S(1)}, s32[]{:S(2)}) async-start(s8[4718592]{0:T(1024)(128)(4,1)} %bitcast.114), calls=%async_computation.13 | async-start | bytes 8388608
  192.1 23.9 %all-to-all-start.1 = ((bf16[16,32,768]{2,1,0:T(8,128)(2,1)}), bf16[16,32,768]{2,1,0:T(8,128)(2,1)S(1)}, u32[]{:S(2)}, u32[]{:S(2)}) async-start(bf16[16,32,768]{2,1,0:T(8,128)(2,1)} %bitcast.109), calls=%async_computation.2 | async-start | bytes 1572864 | tf_op jit(solution)/shard_map/all_to_all | solution.py:176
  216.0 23.5 %all-to-all-start.3 = ((bf16[16,32,768]{2,1,0:T(8,128)(2,1)}), bf16[16,32,768]{2,1,0:T(8,128)(2,1)S(1)}, u32[]{:S(2)}, u32[]{:S(2)}) async-start(bf16[16,32,768]{2,1,0:T(8,128)(2,1)} %bitcast.108), calls=%async_computation.5 | async-start | bytes 1572864 | tf_op jit(solution)/shard_map/all_to_all | solution.py:189
  220.9 174.0 %all-reduce.10.cloned.1.call-start = ((), (), s32[]{:S(2)}) async-start(), calls=%async_computation.10 | async-start | bytes 196608 | tf_op jit(solution)/shard_map/psum | solution.py:252
  232.8 15.6 %copy-start.4 = (f32[197,768]{1,0:T(8,128)S(1)}, f32[197,768]{1,0:T(8,128)}, u32[]{:S(2)}) copy-start(f32[197,768]{1,0:T(8,128)} %copy-done.3) | copy-start | bytes 1815556
  274.9 307.1 %all-reduce.12.cloned.1.call-start = ((), (), s32[]{:S(2)}) async-start(), calls=%async_computation.11 | async-start | bytes 9437184 | tf_op jit(solution)/shard_map/psum | solution.py:251
  291.8 14.7 %copy-start.6 = (bf16[197,768]{1,0:T(8,128)(2,1)S(1)}, bf16[197,768]{1,0:T(8,128)(2,1)}, u32[]{:S(2)}) copy-start(bf16[197,768]{1,0:T(8,128)(2,1)} %param.12) | copy-start | bytes 907780
  291.8 14.7 %copy-start.27 = (f32[768]{0:T(1024)S(1)}, f32[768]{0:T(1024)}, u32[]{:S(2)}) copy-start(f32[768]{0:T(1024)} %param.13) | copy-start | bytes 9220
  291.8 14.7 %copy-start.30 = (f32[197]{0:T(256)S(1)}, f32[197]{0:T(256)}, u32[]{:S(2)}) copy-start(f32[197]{0:T(256)} %copy-done.29) | copy-start | bytes 2368
  291.8 15.0 %copy-start.38 = (f32[197]{0:T(256)S(1)}, f32[197]{0:T(256)}, u32[]{:S(2)}) copy-start(f32[197]{0:T(256)} %copy-done.37) | copy-start | bytes 2368
  291.8 15.0 %copy-start.33 = (f32[197]{0:T(256)S(1)}, f32[197]{0:T(256)}, u32[]{:S(2)}) copy-start(f32[197]{0:T(256)} %copy-done.32) | copy-start | bytes 2368
  291.8 55.6 %copy-start.8 = (f32[197,768]{1,0:T(8,128)S(1)}, f32[197,768]{1,0:T(8,128)}, u32[]{:S(2)}) copy-start(f32[197,768]{1,0:T(8,128)} %copy-done.7) | copy-start | bytes 1815556
  291.8 12.5 %collective-permute-start.1 = (bf16[3,768]{1,0:T(4,128)(2,1)S(1)}, bf16[3,768]{1,0:T(4,128)(2,1)S(1)}, u32[]{:S(2)}, u32[]{:S(2)}) collective-permute-start(bf16[3,768]{1,0:T(4,128)(2,1)S(1)} %slice.34), channel_id=1, source_target_pairs={{0,1},{2,3},{4,5},{6,7},{8,9},{10,11},{12,13},{14,15},{16,17},{18,... | collective-permute-start | bytes 13832
  (27 other events, 107.2 us)
Sparse Core Ops, SparseCore 0:
  87.9 9.0 all-gather.4
  115.8 9.0 all-gather.6
  162.4 8.3 reduce-scatter.6
  192.2 8.5 reduce-scatter.8
  275.0 119.7 all-reduce.9
  401.0 180.9 all-reduce.11
where the time goes:
time: 605 us; the launch traced here: 595 us
  waiting for transfers between devices  292 us (48%)
  matrix products  103 us (17%)
  local copies, waits for them, and re-layouts  68.5 us (11%)
  blocking collectives  53.4 us (9%)
  starting transfers between devices  36.9 us (6%)
  other arithmetic  25.5 us (4%)
  between operations  16.1 us (3%)
    psum x1, waiting for transfers between devices, body(): qkv_grad, out_grad = lax.psum((qkv_grad, out_grad), 'rows')  187 us
    psum x1, waiting for transfers between devices, body(): lax.psum((router_grad, ln1_gain_grad, ln1_shift_grad, ln2_gain_grad, ln2_...  46.3 us
    psum x1, blocking collectives, body(): lax.psum((router_grad, ln1_gain_grad, ln1_shift_grad, ln2_gain_grad, ln2_...  40.2 us
    dot_general x1, matrix products, body(): jnp.dot(both_rows, expert_in, preferred_element_type=jnp.float32) * mask  35.3 us
    unnamed x108, local copies, waits for them, and re-layouts  30.5 us
    dot_general x5, matrix products, dot_rows(): lax.dot_general(first_side, second_side, (((0,), (0,)), ((), ())), prefer...  26.8 us
    dot_general x5, matrix products, dot_last(): lax.dot_general(first_side, second_side, (((1,), (1,)), ((), ())), prefer...  22.5 us
    all_to_all x1, waiting for transfers between devices, body(): lax.all_to_all(grads_send.reshape(row_count, slots, model_width), 'rows',...  18.6 us
  transfers between devices with their start and end apart: 12, of which 7 were waited for; matrix products, arithmetic and copies ran while one was open for 19% of the time, Pallas kernels for 0%

commit v1 on v0

v1 whole, which is shorter than its diff:
```python
import jax
import jax.numpy as jnp
from jax import lax
from jax.experimental import pallas as pl
from jax.experimental.pallas import tpu as pltpu
from jax.sharding import PartitionSpec as P

DH = 64
FF = 3072
SEQ = 197


EPSILON = 1e-06


def layer_norm(values, norm_gain, norm_shift):
    average = jnp.mean(values, axis=-1, keepdims=True)
    centred = values - average
    variance = jnp.mean(centred * centred, axis=-1, keepdims=True)
    return centred * lax.rsqrt(variance + EPSILON) * norm_gain + norm_shift


def gelu_slope(pre_act):
    normal_cdf = 0.5 * (1.0 + jax.scipy.special.erf(pre_act * 0.7071067811865476))
    density = jnp.exp(-0.5 * pre_act * pre_act) * 0.3989422804014327
    return normal_cdf + pre_act * density


def dot_rows(first_side, second_side):
    return lax.dot_general(
        first_side, second_side, (((0,), (0,)), ((), ())), preferred_element_type=jnp.float32
    )


def dot_last(first_side, second_side):
    return lax.dot_general(
        first_side, second_side, (((1,), (1,)), ((), ())), preferred_element_type=jnp.float32
    )


def bit_orders(bits):
    cycle = list(range(bits - 1))
    return [cycle[turn:] + cycle[:turn] + [bits - 1] for turn in range(3)]


def sum_kernel(
    qkv_ref,
    out_ref,
    small_ref,
    qkv_sum,
    out_sum,
    small_sum,
    qkv_acc,
    out_acc,
    qkv_got,
    out_got,
    small_acc,
    small_got,
    send_sems,
    recv_sems,
    small_send,
    small_recv,
):
    shards = qkv_ref.shape[0]
    bits = shards.bit_length() - 1
    row_place = lax.axis_index("rows")
    col_place = lax.axis_index("cols")

    def row_partner(bit):
        here = (row_place // 2**bit) % 2
        return here, (row_place + (1 - 2 * here) * 2**bit, col_place)

    other_core = (row_place, 1 - col_place)
    barrier = pltpu.get_barrier_semaphore()
    for bit in range(bits):
        pl.semaphore_signal(
            barrier, inc=1, device_id=row_partner(bit)[1], device_id_type=pl.DeviceIdType.MESH
        )
    pl.semaphore_signal(
        barrier, inc=1, device_id=other_core, device_id_type=pl.DeviceIdType.MESH
    )
    pl.semaphore_wait(barrier, bits + 1)

    width = qkv_ref.shape[2]
    third = (width * qkv_ref.shape[1] + out_ref.shape[2] * out_ref.shape[1]) // (
        3 * qkv_ref.shape[1]
    )
    third = min(third // 128 * 128, width // 2)
    orders = bit_orders(bits)
    streams = [
        (qkv_ref, qkv_acc, qkv_got, qkv_sum, pl.ds(0, third), orders[0]),
        (qkv_ref, qkv_acc, qkv_got, qkv_sum, pl.ds(third, third), orders[1]),
        (out_ref, out_acc, out_got, out_sum, pl.ds(0, out_ref.shape[2]), orders[2]),
    ]
    if width > 2 * third:
        last = pl.ds(2 * third, width - 2 * third)
        streams.append((qkv_ref, qkv_acc, qkv_got, qkv_sum, last, orders[2]))
    bases = [0 for unused in streams]

    def send(source, target, place, step, device):
        copy = pltpu.make_async_remote_copy(
            src_ref=source,
            dst_ref=target,
            send_sem=send_sems.at[place, step],
            recv_sem=recv_sems.at[place, step],
            device_id=device,
            device_id_type=pl.DeviceIdType.MESH,
        )
        copy.start()
        return copy

    small_acc[0] = small_ref[...]

    def small_send_start(step):
        device = row_partner(step)[1] if step < bits else other_core
        copy = pltpu.make_async_remote_copy(
            src_ref=small_acc.at[step],
            dst_ref=small_got.at[step],
            send_sem=small_send.at[step],
            recv_sem=small_recv.at[step],
            device_id=device,
            device_id_type=pl.DeviceIdType.MESH,
        )
        copy.start()
        return copy

    def small_finish(step, copy):
        copy.wait()
        small_acc[step + 1] = small_acc[step] + small_got[step]

    got_base = 0
    half = shards
    for step in range(bits):
        half = half // 2
        copies = []
        for place, (ref, acc, got, total, cols, order) in enumerate(streams):
            here, device = row_partner(order[step])
            source = ref if step == 0 else acc
            give = bases[place] + (1 - here) * half
            bases[place] = bases[place] + here * half
            copies.append(
                send(
                    source.at[pl.ds(give, half), :, cols],
                    got.at[pl.ds(got_base, half), :, cols],
                    place,
                    step,
                    device,
                )
            )
        small_copy = small_send_start(step)
        for place, (ref, acc, got, total, cols, order) in enumerate(streams):
            copies[place].wait()
            source = ref if step == 0 else acc
            keep = bases[place]

            def add(index, unused, source=source, acc=acc, got=got, cols=cols, keep=keep, start=got_base):
                acc[keep + index, :, cols] = (
                    source[keep + index, :, cols].astype(jnp.float32)
                    + got[start + index, :, cols].astype(jnp.float32)
                ).astype(jnp.bfloat16)
                return unused

            lax.fori_loop(0, half, add, 0)
        small_finish(step, small_copy)
        got_base += half
    small_copy = small_send_start(bits)
    for place, (ref, acc, got, total, cols, order) in enumerate(streams):
        total[bases[place], :, cols] = acc[bases[place], :, cols]
    held = 1
    for step in reversed(range(bits)):
        copies = []
        for place, (ref, acc, got, total, cols, order) in enumerate(streams):
            here, device = row_partner(order[step])
            block = total.at[pl.ds(bases[place], held), :, cols]
            copies.append(send(block, block, place, 2 * bits - 1 - step, device))
            bases[place] = bases[place] - here * held
        for copy in copies:
            copy.wait()
        held = 2 * held
    small_finish(bits, small_copy)
    small_sum[...] = small_acc[bits + 1]


def sum_over_devices(qkv_part, out_part, small_part):
    shards = lax.axis_size("rows")
    bits = shards.bit_length() - 1
    qkv_shape = (shards, qkv_part.shape[0] // shards, qkv_part.shape[1])
    out_shape = (shards, out_part.shape[0] // shards, out_part.shape[1])
    small_shape = small_part.shape
    in_vmem = pl.BlockSpec(memory_space=pltpu.VMEM)
    qkv_sum, out_sum, small_sum = pl.pallas_call(
        sum_kernel,
        out_shape=(
            jax.ShapeDtypeStruct(qkv_shape, jnp.bfloat16),
            jax.ShapeDtypeStruct(out_shape, jnp.bfloat16),
            jax.ShapeDtypeStruct(small_shape, jnp.float32),
        ),
        in_specs=[in_vmem] * 3,
        out_specs=(in_vmem,) * 3,
        scratch_shapes=[
            pltpu.VMEM(qkv_shape, jnp.bfloat16),
            pltpu.VMEM(out_shape, jnp.bfloat16),
            pltpu.VMEM(qkv_shape, jnp.bfloat16),
            pltpu.VMEM(out_shape, jnp.bfloat16),
            pltpu.VMEM((bits + 2, *small_shape), jnp.float32),
            pltpu.VMEM((bits + 1, *small_shape), jnp.float32),
            pltpu.SemaphoreType.DMA((4, 2 * bits)),
            pltpu.SemaphoreType.DMA((4, 2 * bits)),
            pltpu.SemaphoreType.DMA((bits + 1,)),
            pltpu.SemaphoreType.DMA((bits + 1,)),
        ],
        compiler_params=pltpu.CompilerParams(collective_id=0, has_side_effects=True),
        name="sum_gradients",
    )(qkv_part.reshape(qkv_shape), out_part.reshape(out_shape), small_part)
    return (
        qkv_sum.astype(jnp.float32).reshape(qkv_part.shape),
        out_sum.astype(jnp.float32).reshape(out_part.shape),
        small_sum,
    )


def attention_scores(queries, keys_all, score_scale):
    scores = jnp.einsum("nqhd,nkhd->nhqk", queries, keys_all, preferred_element_type=jnp.float32)
    return scores * score_scale


def share_over_cores(parts, col_place):
    theirs = lax.dynamic_index_in_dim(parts, 1 - col_place, 0, keepdims=False)
    ours = lax.dynamic_index_in_dim(parts, col_place, 0, keepdims=False)
    return ours, lax.ppermute(theirs, "cols", [(0, 1), (1, 0)])


def body(
    tokens_in,
    ln1_gain,
    ln1_shift,
    qkv_weight,
    out_weight,
    ln2_gain,
    ln2_shift,
    router_weight,
    expert_in,
    expert_out,
    routes,
    cotangent,
):
    local_rows = tokens_in.shape[0]
    model_width = tokens_in.shape[1]
    experts = router_weight.shape[1]
    capacity = max(2, 8 * local_rows // (3 * experts))
    heads_local = qkv_weight.shape[1] // (3 * DH)
    score_scale = DH ** (-0.5)
    row_place = lax.axis_index("rows")
    col_place = lax.axis_index("cols")
    device_count = lax.axis_size("rows") * lax.axis_size("cols")
    copies = device_count // experts
    slot_ids = jnp.arange(device_count * capacity, dtype=jnp.int32)
    slot_expert = slot_ids // (capacity * copies)
    names_slot = [routes[:, k][:, None] == slot_expert[None, :] for k in range(2)]
    token_ids = jnp.arange(local_rows, dtype=jnp.int32)
    earlier = (token_ids[None, :] < token_ids[:, None]).astype(jnp.bfloat16)
    slot_ranks = jnp.dot(
        earlier,
        (names_slot[0] | names_slot[1]).astype(jnp.bfloat16),
        preferred_element_type=jnp.float32,
    )
    in_slot = slot_ranks == (slot_ids % capacity).astype(jnp.float32)[None, :]
    place_one = (names_slot[0] & in_slot).astype(jnp.bfloat16)
    place_two = (names_slot[1] & in_slot).astype(jnp.bfloat16)
    place_any = place_one + place_two

    def to_experts(token_rows):
        filled = dot_rows(place_any, token_rows).astype(jnp.bfloat16)
        return swap_slots(filled)

    def swap_slots(slot_rows):
        swapped = lax.all_to_all(
            slot_rows.reshape(device_count, capacity, model_width),
            ("rows", "cols"),
            split_axis=0,
            concat_axis=0,
            tiled=True,
        )
        return swapped.reshape(device_count * capacity, model_width)

    cotangent_arrived = to_experts(cotangent)
    tokens_f = tokens_in.astype(jnp.float32)
    normed_low = layer_norm(tokens_f, ln1_gain, ln1_shift).astype(jnp.bfloat16)
    gathered = lax.all_gather(normed_low, "cols", axis=0, tiled=True)
    pair_rows = gathered.shape[0]
    images = pair_rows // SEQ
    qkv_low = jnp.dot(gathered, qkv_weight, preferred_element_type=jnp.float32).astype(jnp.bfloat16)
    head_split = qkv_low.reshape(images, SEQ, heads_local, 3, DH)
    queries = head_split[:, :, :, 0]
    keys_all = head_split[:, :, :, 1]
    values_all = head_split[:, :, :, 2]
    scores = attention_scores(queries, keys_all, score_scale)
    score_peak = jnp.max(scores, axis=-1, keepdims=True)
    log_total = score_peak + jnp.log(jnp.sum(jnp.exp(scores - score_peak), axis=-1, keepdims=True))
    weights_low = jnp.exp(scores - log_total).astype(jnp.bfloat16)
    context = jnp.einsum(
        "nhqk,nkhd->nqhd", weights_low, values_all, preferred_element_type=jnp.float32
    )
    context_low = context.astype(jnp.bfloat16).reshape(pair_rows, heads_local * DH)
    attn_parts = jnp.dot(context_low, out_weight, preferred_element_type=jnp.float32)
    attn_ours, attn_theirs = share_over_cores(
        attn_parts.reshape(images, SEQ, model_width), col_place
    )
    attn_out = attn_ours + attn_theirs
    hidden_one = tokens_f + attn_out
    mixed_low = layer_norm(hidden_one, ln2_gain, ln2_shift).astype(jnp.bfloat16)
    logits = jnp.dot(mixed_low, router_weight, preferred_element_type=jnp.float32)
    router_probs = jax.nn.softmax(logits, axis=-1)
    expert_ids = jnp.arange(experts, dtype=jnp.int32)
    chosen = (routes[:, :, None] == expert_ids[None, None, :]).astype(jnp.float32)
    gate_values = jnp.sum(router_probs[:, None, :] * chosen, axis=-1)
    grad_out = cotangent.astype(jnp.float32)
    arrived = to_experts(mixed_low)
    own_expert = (row_place * lax.axis_size("cols") + col_place) // copies
    arrived_probs = jax.nn.softmax(
        jnp.dot(arrived, router_weight, preferred_element_type=jnp.float32), axis=-1
    )
    arrived_gate = jnp.sum(
        jnp.where(expert_ids[None, :] == own_expert, arrived_probs, 0.0), axis=-1, keepdims=True
    )
    grad_result = (arrived_gate * cotangent_arrived.astype(jnp.float32)).astype(jnp.bfloat16)
    pre_act = jnp.dot(arrived, expert_in, preferred_element_type=jnp.float32)
    act_low = jax.nn.gelu(pre_act, approximate=False).astype(jnp.bfloat16)
    result_low = jnp.dot(act_low, expert_out, preferred_element_type=jnp.float32).astype(
        jnp.bfloat16
    )
    returned = swap_slots(result_low)
    grad_act = dot_last(grad_result, expert_out)
    grad_pre_low = (grad_act * gelu_slope(pre_act)).astype(jnp.bfloat16)
    grad_arrived = dot_last(grad_pre_low, expert_in).astype(jnp.bfloat16)
    grad_sent = swap_slots(grad_arrived)
    first_grad = dot_rows(arrived, grad_pre_low)
    second_grad = dot_rows(act_low, grad_result)
    picked_one = jnp.dot(place_one, returned, preferred_element_type=jnp.float32)
    picked_two = jnp.dot(place_two, returned, preferred_element_type=jnp.float32)
    output = (
        hidden_one + gate_values[:, 0:1] * picked_one + gate_values[:, 1:2] * picked_two
    ).astype(jnp.bfloat16)
    grad_gates = jnp.stack(
        [jnp.sum(grad_out * picked_one, axis=-1), jnp.sum(grad_out * picked_two, axis=-1)], axis=1
    )
    grad_mixed_experts = jnp.dot(place_any, grad_sent, preferred_element_type=jnp.float32)
    gate_term = jnp.sum(grad_gates * gate_values, axis=-1, keepdims=True)
    grad_probs = jnp.sum(chosen * grad_gates[:, :, None], axis=1)
    grad_logits_low = (router_probs * (grad_probs - gate_term)).astype(jnp.bfloat16)
    router_grad = dot_rows(grad_logits_low, mixed_low)
    grad_mixed = dot_last(grad_logits_low, router_weight) + grad_mixed_experts
    unused_two, norm_two_back = jax.vjp(layer_norm, hidden_one, ln2_gain, ln2_shift)
    grad_hidden_part, ln2_gain_grad, ln2_shift_grad = norm_two_back(grad_mixed)
    grad_hidden = grad_out + grad_hidden_part
    grad_attn_low = grad_hidden.astype(jnp.bfloat16)
    grad_attn_all = lax.all_gather(grad_attn_low, "cols", axis=0, tiled=True)
    out_grad = dot_rows(context_low, grad_attn_all)
    grad_context = (
        dot_last(grad_attn_all, out_weight)
        .astype(jnp.bfloat16)
        .reshape(images, SEQ, heads_local, DH)
    )
    scores_again = attention_scores(queries, keys_all, score_scale)
    attn_probs = jnp.exp(scores_again - log_total)
    probs_low = attn_probs.astype(jnp.bfloat16)
    grad_values = jnp.einsum(
        "nhqk,nqhd->nkhd", probs_low, grad_context, preferred_element_type=jnp.float32
    )
    grad_weights = jnp.einsum(
        "nqhd,nkhd->nhqk", grad_context, values_all, preferred_element_type=jnp.float32
    )
    row_term = jnp.sum(grad_weights * attn_probs, axis=-1, keepdims=True)
    grad_scores = (attn_probs * (grad_weights - row_term)).astype(jnp.bfloat16)
    grad_queries = (
        jnp.einsum("nhqk,nkhd->nqhd", grad_scores, keys_all, preferred_element_type=jnp.float32)
        * score_scale
    )
    grad_keys = (
        jnp.einsum("nhqk,nqhd->nkhd", grad_scores, queries, preferred_element_type=jnp.float32)
        * score_scale
    )
    grad_qkv = (
        jnp.stack([grad_queries, grad_keys, grad_values], axis=3)
        .astype(jnp.bfloat16)
        .reshape(pair_rows, 3 * heads_local * DH)
    )
    qkv_grad = dot_rows(gathered, grad_qkv)
    normed_ours, normed_theirs = share_over_cores(
        dot_last(grad_qkv, qkv_weight).astype(jnp.bfloat16).reshape(images, SEQ, model_width),
        col_place,
    )
    grad_normed = normed_ours.astype(jnp.float32) + normed_theirs.astype(jnp.float32)
    unused_one, norm_one_back = jax.vjp(layer_norm, tokens_f, ln1_gain, ln1_shift)
    grad_tokens_part, ln1_gain_grad, ln1_shift_grad = norm_one_back(grad_normed)
    tokens_grad = (grad_hidden + grad_tokens_part).astype(jnp.bfloat16)
    small_part = jnp.concatenate(
        [
            router_grad,
            ln1_gain_grad[None],
            ln1_shift_grad[None],
            ln2_gain_grad[None],
            ln2_shift_grad[None],
            jnp.zeros((4, model_width), jnp.float32),
        ],
        axis=0,
    )
    qkv_grad, out_grad, small_sum = sum_over_devices(
        qkv_grad.astype(jnp.bfloat16), out_grad.astype(jnp.bfloat16), small_part
    )
    router_grad = small_sum[:experts].T
    ln1_gain_grad, ln1_shift_grad, ln2_gain_grad, ln2_shift_grad = (
        small_sum[experts],
        small_sum[experts + 1],
        small_sum[experts + 2],
        small_sum[experts + 3],
    )
    return (
        output,
        tokens_grad,
        ln1_gain_grad,
        ln1_shift_grad,
        qkv_grad,
        out_grad,
        ln2_gain_grad,
        ln2_shift_grad,
        router_grad,
        first_grad,
        second_grad,
    )


def solution(mesh):
    in_specs = (
        P(("rows", "cols"), None),
        P(),
        P(),
        P(None, "cols"),
        P("cols", None),
        P(),
        P(),
        P(),
        P(None, ("rows", "cols")),
        P(("rows", "cols"), None),
        P(("rows", "cols"), None),
        P(("rows", "cols"), None),
    )
    out_specs = (
        P(("rows", "cols"), None),
        P(("rows", "cols"), None),
        P(),
        P(),
        P(None, "cols"),
        P("cols", None),
        P(),
        P(),
        P(),
        P(None, ("rows", "cols")),
        P(("rows", "cols"), None),
    )
    return jax.shard_map(body, mesh=mesh, in_specs=in_specs, out_specs=out_specs, check_vma=False)
```

time: 605 us -> 268 us (0.44); the launches traced: 595 us -> 267 us
  waiting for transfers between devices: 292 us -> 25.1 us
  Pallas kernels: 0 us -> 68.8 us
  blocking collectives: 53.4 us -> 4.96 us
  local copies, waits for them, and re-layouts: 68.5 us -> 41.5 us
  matrix products: 103 us -> 79.8 us
  between operations: 16.1 us -> 1.36 us
  starting transfers between devices: 36.9 us -> 23.4 us
    psum x2 -> x0, waiting for transfers between devices: 233 us -> none  [the longest x1 187 us: body(): qkv_grad, out_grad = lax.psum((qkv_grad, out_grad), 'rows')]
    pallas_call x0 -> x1, Pallas kernels: none -> 68.8 us  [sum_over_devices(): pl.pallas_call(sum_kernel, out_shape=(jax.ShapeDtypeStruct(qkv_shape, jnp...]
    psum x1 -> x0, blocking collectives: 40.2 us -> none  [body(): lax.psum((router_grad, ln1_gain_grad, ln1_shift_grad, ln2_gain_grad, ln2_...]
    all_to_all x4, waiting for transfers between devices: 54.6 us -> 23.9 us  [swap_slots(): lax.all_to_all(slot_rows.reshape(device_count, capacity, model_width), ('...]
    unnamed x108 -> x95, local copies, waits for them, and re-layouts: 30.5 us -> 15.8 us
    dot_general x2 -> x7, matrix products: 37 us -> 25 us  [the longest x1 17.8 us: body(): pre_act = jnp.dot(arrived, expert_in, preferred_element_type=jnp.float32)]
    reduce_scatter x2 -> x0, starting transfers between devices: 8.79 us -> none  [the longest x1 8.75 us: body(): lax.psum_scatter(dot_last(grad_pre_low, expert_in).astype(jnp.bfloat16),...]
    unnamed x2 -> x0, blocking collectives: 8.31 us -> none
  transfers between devices with their start and end apart: 12 -> 6, of which waited for: 7 -> 3; matrix products, arithmetic and copies ran while one was open for 19% -> 26% of each run, Pallas kernels for 0% -> 0%
where the time goes in v1:
time: 268 us; the launch traced here: 267 us
  matrix products  79.8 us (30%)
  Pallas kernels  68.8 us (26%)
  local copies, waits for them, and re-layouts  41.5 us (15%)
  waiting for transfers between devices  25.1 us (9%)
  starting transfers between devices  23.4 us (9%)
  other arithmetic  21.6 us (8%)
  blocking collectives  4.96 us (2%)
    pallas_call x1, Pallas kernels, sum_over_devices(): pl.pallas_call(sum_kernel, out_shape=(jax.ShapeDtypeStruct(qkv_shape, jnp...  68.8 us
    all_to_all x4, waiting for transfers between devices, swap_slots(): lax.all_to_all(slot_rows.reshape(device_count, capacity, model_width), ('...  23.9 us
    all_to_all x4, starting transfers between devices, swap_slots(): lax.all_to_all(slot_rows.reshape(device_count, capacity, model_width), ('...  22.7 us
    dot_general x7, matrix products, dot_rows(): lax.dot_general(first_side, second_side, (((0,), (0,)), ((), ())), prefer...  21.2 us
    dot_general x1, matrix products, body(): pre_act = jnp.dot(arrived, expert_in, preferred_element_type=jnp.float32)  17.8 us
    dot_general x5, matrix products, dot_last(): lax.dot_general(first_side, second_side, (((1,), (1,)), ((), ())), prefer...  16.5 us
    unnamed x95, local copies, waits for them, and re-layouts  15.8 us
    slice x1, local copies, waits for them, and re-layouts, body(): queries = head_split[:, :, :, 0]  6.89 us
  transfers between devices with their start and end apart: 6, of which 3 were waited for; matrix products, arithmetic and copies ran while one was open for 26% of the time, Pallas kernels for 0%

profile of v1, /device:TPU:0, one launch (start us, length us, event | category | flops | bytes accessed | tf_op | source)
XLA Modules:
  0.0 266.6 jit_solution(5683443856038633343)
XLA Ops:
  4.3 2.3 all-gather
  7.6 2.0 convolution_convert_fusion.1
  9.6 2.9 %reshape.235 = bf16[2,197,6,3,64]{4,3,2,1,0:T(4,128)(2,1)} reshape(bf16[394,1152]{1,0:T(8,128)(2,1)S(1)} %convolution_convert_fusion.1) | data formatting | bytes 1815552 | tf_op jit(solution)/shard_map/reshape | solution.py:293
  12.5 6.9 %fusion.85 = (bf16[2,197,6,1,64]{4,3,2,1,0:T(2,128)(2,1)}, bf16[2,197,6,1,64]{4,3,2,1,0:T(2,128)(2,1)}, bf16[2,197,6,1,64]{4,3,2,1,0:T(2,128)(2,1)S(1)}) fusion(bf16[2,197,6,3,64]{4,3,2,1,0:T(4,128)(2,1)} %reshape.235), kind=kLoop, calls=%fused_computation.164 | loop fusion | bytes 1815552 | tf_op jit(solution)/shard_map/slice | solution.py:294
  19.4 3.5 %copy.93 = bf16[2,197,6,1,64]{1,4,2,0,3:T(8,128)(2,1)} copy(bf16[2,197,6,1,64]{4,3,2,1,0:T(2,128)(2,1)} %get-tuple-element.35) | data formatting | bytes 605184
  23.0 3.5 %copy.92 = bf16[2,197,6,1,64]{1,4,2,0,3:T(8,128)(2,1)} copy(bf16[2,197,6,1,64]{4,3,2,1,0:T(2,128)(2,1)} %get-tuple-element.36) | data formatting | bytes 605184
  26.5 2.0 copy.94
  32.2 2.3 convolution_convert_fusion.9
  42.2 7.2 %all-to-all-start = ((bf16[32,16,768]{2,1,0:T(8,128)(2,1)}), bf16[32,16,768]{2,1,0:T(8,128)(2,1)S(1)}, u32[]{:S(2)}, u32[]{:S(2)}) async-start(bf16[32,16,768]{2,1,0:T(8,128)(2,1)} %bitcast.138), calls=%async_computation | async-start | bytes 1572864 | tf_op jit(solution)/shard_map/all_to_all | solution.py:277
  49.4 2.1 copy.82
  54.1 2.5 convolution_convert_fusion.3
  58.4 11.6 %all-to-all-done = bf16[32,16,768]{2,1,0:T(8,128)(2,1)S(1)} async-done(((bf16[32,16,768]{2,1,0:T(8,128)(2,1)}), bf16[32,16,768]{2,1,0:T(8,128)(2,1)S(1)}, u32[]{:S(2)}, u32[]{:S(2)}) %all-to-all-start) | async-done | bytes 786464 | tf_op jit(solution)/shard_map/all_to_all | solution.py:277
  70.0 3.9 %all-to-all-start.2 = ((bf16[32,16,768]{2,1,0:T(8,128)(2,1)}), bf16[32,16,768]{2,1,0:T(8,128)(2,1)}, u32[]{:S(2)}, u32[]{:S(2)}) async-start(bf16[32,16,768]{2,1,0:T(8,128)(2,1)} %bitcast.139), calls=%async_computation.2 | async-start | bytes 1572864 | tf_op jit(solution)/shard_map/all_to_all | solution.py:277
  74.0 17.8 %fusion.2 = (bf16[512,3072]{1,0:T(8,128)(2,1)S(1)}, f32[512,3072]{1,0:T(8,128)}) fusion(bf16[512,768]{1,0:T(8,128)(2,1)S(1)} %bitcast.132, bf16[768,3072]{1,0:T(8,128)(2,1)} %param.20), kind=kOutput, calls=%fused_computation.4 | convolution fusion | flops 2518155264 | bytes 14942208 | tf_op jit(solution)/shard_map/dot_general | solution.py:327
  93.4 5.8 %convolution_convert_fusion.4 = bf16[512,768]{1,0:T(8,128)(2,1)} fusion(bf16[512,3072]{1,0:T(8,128)(2,1)S(1)} %get-tuple-element.47, bf16[3072,768]{1,0:T(8,128)(2,1)} %param.21), kind=kOutput, calls=%fused_computation.39 | convolution fusion | flops 2416312320 | bytes 8650752 | tf_op jit(solution)/shard_map/dot_general | solution.py:329
  99.3 5.9 %all-to-all-start.1 = ((bf16[32,16,768]{2,1,0:T(8,128)(2,1)}), bf16[32,16,768]{2,1,0:T(8,128)(2,1)}, u32[]{:S(2)}, u32[]{:S(2)}) async-start(bf16[32,16,768]{2,1,0:T(8,128)(2,1)} %bitcast.140), calls=%async_computation.1 | async-start | bytes 1572864 | tf_op jit(solution)/shard_map/all_to_all | solution.py:277
  106.5 6.8 %fusion.8 = bf16[512,3072]{1,0:T(8,128)(2,1)S(1)} fusion(f32[512,3072]{1,0:T(8,128)} %get-tuple-element.48, bf16[512,768]{1,0:T(8,128)(2,1)S(1)} %fusion.17, bf16[3072,768]{1,0:T(8,128)(2,1)} %param.21), kind=kOutput, calls=%fused_computation.10 | convolution fusion | flops 2431647744 | bytes 14942208 | tf_op jit(solution)/shard_map/dot_general | solution.py:36
  113.4 5.2 %fusion.93 = f32[3072,768]{1,0:T(8,128)} fusion(bf16[512,3072]{1,0:T(8,128)(2,1)S(1)} %copy-done.42, bf16[512,768]{1,0:T(8,128)(2,1)S(1)} %fusion.17), kind=kOutput, calls=%fused_computation.172 | convolution fusion | flops 2415919104 | bytes 13369344 | tf_op jit(solution)/shard_map/dot_general | solution.py:30
  118.6 5.2 %fusion.92 = f32[768,3072]{1,0:T(8,128)} fusion(bf16[512,768]{1,0:T(8,128)(2,1)S(1)} %bitcast.134, bf16[512,3072]{1,0:T(8,128)(2,1)S(1)} %fusion.8), kind=kOutput, calls=%fused_computation.171 | convolution fusion | flops 2415919104 | bytes 13369344 | tf_op jit(solution)/shard_map/dot_general | solution.py:30
  123.8 3.5 %convolution_convert_fusion.2 = bf16[512,768]{1,0:T(8,128)(2,1)} fusion(bf16[512,3072]{1,0:T(8,128)(2,1)S(1)} %fusion.8, bf16[768,3072]{1,0:T(8,128)(2,1)S(1)} %bitcast.159), kind=kOutput, calls=%fused_computation.37 | convolution fusion | flops 2416312320 | bytes 8650752 | tf_op jit(solution)/shard_map/dot_general | solution.py:36
  127.3 5.7 %all-to-all-start.3 = ((bf16[32,16,768]{2,1,0:T(8,128)(2,1)}), bf16[32,16,768]{2,1,0:T(8,128)(2,1)}, u32[]{:S(2)}, u32[]{:S(2)}) async-start(bf16[32,16,768]{2,1,0:T(8,128)(2,1)} %bitcast.21), calls=%async_computation.3 | async-start | bytes 1572864 | tf_op jit(solution)/shard_map/all_to_all | solution.py:277
  134.5 2.5 fusion.34
  141.3 12.3 %all-to-all-done.3 = bf16[32,16,768]{2,1,0:T(8,128)(2,1)} async-done(((bf16[32,16,768]{2,1,0:T(8,128)(2,1)}), bf16[32,16,768]{2,1,0:T(8,128)(2,1)}, u32[]{:S(2)}, u32[]{:S(2)}) %all-to-all-start.3) | async-done | bytes 786464 | tf_op jit(solution)/shard_map/all_to_all | solution.py:277
  153.6 2.0 multiply_reduce_fusion.2
  156.3 2.2 fusion.83
  159.5 2.6 all-gather.1
  167.7 2.4 fusion.20
  176.8 3.4 %convolution_convert_fusion.6 = bf16[394,768]{1,0:T(8,128)(2,1)} fusion(bf16[394,1152]{0,1:T(8,128)(2,1)} %convert_element_type.136, bf16[768,1152]{1,0:T(8,128)(2,1)S(1)} %copy-done), kind=kOutput, calls=%fused_computation.41 | convolution fusion | flops 697474560 | bytes 3282432 | tf_op jit(solution)/shard_map/dot_general | solution.py:36
  181.6 3.8 %convolution_convert_fusion = bf16[768,1152]{1,0:T(8,128)(2,1)} fusion(bf16[394,768]{1,0:T(8,128)(2,1)S(1)} %copy-done.17, bf16[394,1152]{0,1:T(8,128)(2,1)} %convert_element_type.136), kind=kOutput, calls=%fused_computation.26 | convolution fusion | flops 698056704 | bytes 3282432 | tf_op jit(solution)/shard_map/dot_general | solution.py:30
  187.9 68.8 %sum_gradients.1 = (bf16[16,48,1152]{2,1,0:T(8,128)(2,1)}, bf16[16,24,768]{2,1,0:T(8,128)(2,1)}, f32[40,768]{1,0:T(8,128)}) custom-call(bf16[16,48,1152]{2,1,0:T(8,128)(2,1)} %bitcast.137, bf16[16,24,768]{2,1,0:T(8,128)(2,1)} %bitcast.141, f32[40,768]{1,0:T(8,128)} %concatenate.3.small_ref), custom_call_target="tpu_custom_call" | custom-call | tf_op jit(solution)/shard_map/sum_gradients/pallas_call | solution.py:191
  259.8 2.2 bitcast_convert_fusion.1
  262.0 3.5 %bitcast_convert_fusion = f32[768,1152]{1,0:T(8,128)} fusion(bf16[16,48,1152]{2,1,0:T(8,128)(2,1)} %get-tuple-element.15), kind=kLoop, calls=%fused_computation.33 | loop fusion | flops 884736 | bytes 5308416 | tf_op jit(solution)/shard_map/reshape | solution.py:216
  (164 shorter events, 50.8 us)
Async XLA Ops:
  0.6 7.0 %copy-start = (bf16[768,1152]{1,0:T(8,128)(2,1)S(1)}, bf16[768,1152]{1,0:T(8,128)(2,1)}, u32[]{:S(2)}) copy-start(bf16[768,1152]{1,0:T(8,128)(2,1)} %param.15) | copy-start | bytes 5308420
  3.1 9.4 %copy-start.30 = (f32[197]{0:T(256)}, f32[197]{0:T(256)S(1)}, u32[]{:S(2)}) copy-start(f32[197]{0:T(256)S(1)} %fusion.32) | copy-start | bytes 2368
  28.5 6.0 %copy-start.19 = (bf16[384,768]{1,0:T(8,128)(2,1)S(1)}, bf16[384,768]{1,0:T(8,128)(2,1)}, u32[]{:S(2)}) copy-start(bf16[384,768]{1,0:T(8,128)(2,1)} %param.16) | copy-start | bytes 1769476
  30.2 6.3 %copy-start.33 = (s32[197,2]{0,1:T(2,128)S(1)}, s32[197,2]{0,1:T(2,128)}, u32[]{:S(2)}) copy-start(s32[197,2]{0,1:T(2,128)} %param.22) | copy-start | bytes 4732
  31.7 6.5 %copy-start.3 = (bf16[197,768]{1,0:T(8,128)(2,1)S(1)}, bf16[197,768]{1,0:T(8,128)(2,1)}, u32[]{:S(2)}) copy-start(bf16[197,768]{1,0:T(8,128)(2,1)} %param.12) | copy-start | bytes 907780
  32.2 7.6 %copy-start.27 = (f32[768]{0:T(1024)S(1)}, f32[768]{0:T(1024)}, u32[]{:S(2)}) copy-start(f32[768]{0:T(1024)} %param.17) | copy-start | bytes 9220
  32.2 7.6 %copy-start.35 = (f32[768]{0:T(1024)S(1)}, f32[768]{0:T(1024)}, u32[]{:S(2)}) copy-start(f32[768]{0:T(1024)} %param.18) | copy-start | bytes 9220
  36.1 2.1 collective-permute-start
  36.6 17.5 %copy-start.36 = (s32[197,1]{0,1:T(1,128)}, s32[197,1]{0,1:T(1,128)S(1)}, u32[]{:S(2)}) copy-start(s32[197,1]{0,1:T(1,128)S(1)} %get-tuple-element.41) | copy-start | bytes 2368
  36.6 17.5 %copy-start.38 = (s32[197,1]{0,1:T(1,128)}, s32[197,1]{0,1:T(1,128)S(1)}, u32[]{:S(2)}) copy-start(s32[197,1]{0,1:T(1,128)S(1)} %get-tuple-element.42) | copy-start | bytes 2368
  39.8 14.3 %copy-start.28 = (f32[197]{0:T(256)}, f32[197]{0:T(256)S(1)}, u32[]{:S(2)}) copy-start(f32[197]{0:T(256)S(1)} %fusion.76) | copy-start | bytes 2368
  42.2 27.9 %all-to-all-start = ((bf16[32,16,768]{2,1,0:T(8,128)(2,1)}), bf16[32,16,768]{2,1,0:T(8,128)(2,1)S(1)}, u32[]{:S(2)}, u32[]{:S(2)}) async-start(bf16[32,16,768]{2,1,0:T(8,128)(2,1)} %bitcast.138), calls=%async_computation | async-start | bytes 1572864 | tf_op jit(solution)/shard_map/all_to_all | solution.py:277
  70.0 29.3 %all-to-all-start.2 = ((bf16[32,16,768]{2,1,0:T(8,128)(2,1)}), bf16[32,16,768]{2,1,0:T(8,128)(2,1)}, u32[]{:S(2)}, u32[]{:S(2)}) async-start(bf16[32,16,768]{2,1,0:T(8,128)(2,1)} %bitcast.139), calls=%async_computation.2 | async-start | bytes 1572864 | tf_op jit(solution)/shard_map/all_to_all | solution.py:277
  73.9 17.8 %copy-start.20 = (bf16[768,32]{0,1:T(8,128)(2,1)S(1)}, bf16[768,32]{0,1:T(8,128)(2,1)}, u32[]{:S(2)}) copy-start(bf16[768,32]{0,1:T(8,128)(2,1)} %param.19) | copy-start | bytes 147460
  74.0 18.2 %copy-start.40 = (pred[32]{0:T(512)(128)(4,1)S(1)}, pred[32]{0:T(512)(128)(4,1)}, u32[]{:S(2)}) copy-start(pred[32]{0:T(512)(128)(4,1)} %iota_compare_fusion.3) | copy-start | bytes 100
  99.3 28.0 %all-to-all-start.1 = ((bf16[32,16,768]{2,1,0:T(8,128)(2,1)}), bf16[32,16,768]{2,1,0:T(8,128)(2,1)}, u32[]{:S(2)}, u32[]{:S(2)}) async-start(bf16[32,16,768]{2,1,0:T(8,128)(2,1)} %bitcast.140), calls=%async_computation.1 | async-start | bytes 1572864 | tf_op jit(solution)/shard_map/all_to_all | solution.py:277
  106.5 6.8 %copy-start.42 = (bf16[512,3072]{1,0:T(8,128)(2,1)S(1)}, bf16[512,3072]{1,0:T(8,128)(2,1)}, u32[]{:S(2)}) copy-start(bf16[512,3072]{1,0:T(8,128)(2,1)} %copy-done.41) | copy-start | bytes 9437188
  106.5 17.2 %slice-start = ((s8[4718592]{0:T(1024)(128)(4,1)}), s8[4194304]{0:T(1024)(128)(4,1)S(1)}, s32[]{:S(2)}) async-start(s8[4718592]{0:T(1024)(128)(4,1)} %bitcast.158), calls=%async_computation.4 | async-start | bytes 8388608
  113.3 10.4 %slice-start.1 = ((s8[4718592]{0:T(1024)(128)(4,1)}), s8[524288]{0:T(1024)(128)(4,1)S(1)}, s32[]{:S(2)}) async-start(s8[4718592]{0:T(1024)(128)(4,1)} %bitcast.158), calls=%async_computation.5 | async-start | bytes 1048576
  123.7 9.3 %copy-start.23 = (pred[197,512]{1,0:T(8,128)(4,1)S(1)}, pred[197,512]{1,0:T(8,128)(4,1)}, u32[]{:S(2)}) copy-start(pred[197,512]{1,0:T(8,128)(4,1)} %copy-done.22) | copy-start | bytes 302596
  123.7 9.3 %copy-start.39 = (s32[197,1]{0,1:T(1,128)S(1)}, s32[197,1]{0,1:T(1,128)}, u32[]{:S(2)}) copy-start(s32[197,1]{0,1:T(1,128)} %copy-done.38) | copy-start | bytes 2368
  123.8 10.8 %copy-start.37 = (s32[197,1]{0,1:T(1,128)S(1)}, s32[197,1]{0,1:T(1,128)}, u32[]{:S(2)}) copy-start(s32[197,1]{0,1:T(1,128)} %copy-done.36) | copy-start | bytes 2368
  127.3 9.7 %copy-start.34 = (s32[197,2]{0,1:T(2,128)S(1)}, s32[197,2]{0,1:T(2,128)}, u32[]{:S(2)}) copy-start(s32[197,2]{0,1:T(2,128)} %param.22) | copy-start | bytes 4732
  127.3 12.9 %copy-start.21 = (bf16[768,32]{0,1:T(8,128)(2,1)S(1)}, bf16[768,32]{0,1:T(8,128)(2,1)}, u32[]{:S(2)}) copy-start(bf16[768,32]{0,1:T(8,128)(2,1)} %param.19) | copy-start | bytes 147460
  127.3 26.3 %copy-start.29 = (f32[197]{0:T(256)S(1)}, f32[197]{0:T(256)}, u32[]{:S(2)}) copy-start(f32[197]{0:T(256)} %copy-done.28) | copy-start | bytes 2368
  127.3 26.3 %all-to-all-start.3 = ((bf16[32,16,768]{2,1,0:T(8,128)(2,1)}), bf16[32,16,768]{2,1,0:T(8,128)(2,1)}, u32[]{:S(2)}, u32[]{:S(2)}) async-start(bf16[32,16,768]{2,1,0:T(8,128)(2,1)} %bitcast.21), calls=%async_computation.3 | async-start | bytes 1572864 | tf_op jit(solution)/shard_map/all_to_all | solution.py:277
  159.5 10.6 %copy-start.8 = (bf16[2,197,6,1,64]{1,4,2,0,3:T(8,128)(2,1)S(1)}, bf16[2,197,6,1,64]{1,4,2,0,3:T(8,128)(2,1)}, u32[]{:S(2)}) copy-start(bf16[2,197,6,1,64]{1,4,2,0,3:T(8,128)(2,1)} %copy.92) | copy-start | bytes 907780
  180.1 6.5 %copy-start.25 = (f32[32,768]{1,0:T(8,128)S(1)}, f32[32,768]{1,0:T(8,128)}, u32[]{:S(2)}) copy-start(f32[32,768]{1,0:T(8,128)} %fusion.91) | copy-start | bytes 294916
  181.4 4.0 %collective-permute-start.1 = (bf16[197,768]{1,0:T(8,128)(2,1)S(1)}, bf16[197,768]{1,0:T(8,128)(2,1)S(1)}, u32[]{:S(2)}, u32[]{:S(2)}) collective-permute-start(bf16[197,768]{1,0:T(8,128)(2,1)S(1)} %dynamic-slice_bitcast_fusion.1), channel_id=1, source_target_pairs={{0,1},{1,0},{2,3},{3,2},{4,5},{5,4},{6,7},{7,6},{8,9},{9,8},{10,11... | collective-permute-start | bytes 907784 | tf_op jit(solution)/shard_map/ppermute | solution.py:230
  187.9 77.6 %copy-start.5 = (f32[197,768]{1,0:T(8,128)S(1)}, f32[197,768]{1,0:T(8,128)}, u32[]{:S(2)}) copy-start(f32[197,768]{1,0:T(8,128)} %copy-done.4) | copy-start | bytes 1815556
  256.7 8.7 %copy-start.13 = (bf16[197,768]{1,0:T(8,128)(2,1)S(1)}, bf16[197,768]{1,0:T(8,128)(2,1)}, u32[]{:S(2)}) copy-start(bf16[197,768]{1,0:T(8,128)(2,1)} %copy-done.12) | copy-start | bytes 907780
  256.7 8.7 %copy-start.16 = (bf16[197,768]{1,0:T(8,128)(2,1)S(1)}, bf16[197,768]{1,0:T(8,128)(2,1)}, u32[]{:S(2)}) copy-start(bf16[197,768]{1,0:T(8,128)(2,1)} %param.23) | copy-start | bytes 907780
  (19 other events, 48.7 us)

commit v2 on v1

--- a/solution.py
+++ b/solution.py
@@ -128,55 +128,59 @@
         copy.wait()
         small_acc[step + 1] = small_acc[step] + small_got[step]
 
-    got_base = 0
-    half = shards
+    def give_half(place, step):
+        ref, acc, got, total, cols, order = streams[place]
+        here, device = row_partner(order[step])
+        half = shards >> (step + 1)
+        source = ref if step == 0 else acc
+        give = bases[place] + (1 - here) * half
+        bases[place] = bases[place] + here * half
+        return send(
+            source.at[pl.ds(give, half), :, cols],
+            got.at[pl.ds(shards - 2 * half, half), :, cols],
+            place,
+            step,
+            device,
+        )
+
+    def pass_block(place, step):
+        ref, acc, got, total, cols, order = streams[place]
+        here, device = row_partner(order[step])
+        held = shards >> (step + 1)
+        block = total.at[pl.ds(bases[place], held), :, cols]
+        bases[place] = bases[place] - here * held
+        return send(block, block, place, 2 * bits - 1 - step, device)
+
+    copies = [give_half(place, 0) for place in range(len(streams))]
+    small_copy = small_send_start(0)
     for step in range(bits):
-        half = half // 2
-        copies = []
-        for place, (ref, acc, got, total, cols, order) in enumerate(streams):
-            here, device = row_partner(order[step])
-            source = ref if step == 0 else acc
-            give = bases[place] + (1 - here) * half
-            bases[place] = bases[place] + here * half
-            copies.append(
-                send(
-                    source.at[pl.ds(give, half), :, cols],
-                    got.at[pl.ds(got_base, half), :, cols],
-                    place,
-                    step,
-                    device,
-                )
-            )
-        small_copy = small_send_start(step)
+        half = shards >> (step + 1)
         for place, (ref, acc, got, total, cols, order) in enumerate(streams):
             copies[place].wait()
             source = ref if step == 0 else acc
+            target = acc if step < bits - 1 else total
             keep = bases[place]
 
-            def add(index, unused, source=source, acc=acc, got=got, cols=cols, keep=keep, start=got_base):
-                acc[keep + index, :, cols] = (
+            def add(index, unused, parts=(source, target, got, cols, keep, shards - 2 * half)):
+                source, target, got, cols, keep, start = parts
+                target[keep + index, :, cols] = (
                     source[keep + index, :, cols].astype(jnp.float32)
                     + got[start + index, :, cols].astype(jnp.float32)
                 ).astype(jnp.bfloat16)
                 return unused
 
             lax.fori_loop(0, half, add, 0)
+            if step < bits - 1:
+                copies[place] = give_half(place, step + 1)
+            else:
+                copies[place] = pass_block(place, step)
         small_finish(step, small_copy)
-        got_base += half
-    small_copy = small_send_start(bits)
-    for place, (ref, acc, got, total, cols, order) in enumerate(streams):
-        total[bases[place], :, cols] = acc[bases[place], :, cols]
-    held = 1
+        small_copy = small_send_start(step + 1)
     for step in reversed(range(bits)):
-        copies = []
-        for place, (ref, acc, got, total, cols, order) in enumerate(streams):
-            here, device = row_partner(order[step])
-            block = total.at[pl.ds(bases[place], held), :, cols]
-            copies.append(send(block, block, place, 2 * bits - 1 - step, device))
-            bases[place] = bases[place] - here * held
-        for copy in copies:
-            copy.wait()
-        held = 2 * held
+        for place in range(len(streams)):
+            copies[place].wait()
+            if step > 0:
+                copies[place] = pass_block(place, step - 1)
     small_finish(bits, small_copy)
     small_sum[...] = small_acc[bits + 1]
 
@@ -219,14 +223,150 @@
     )
 
 
-def attention_scores(queries, keys_all, score_scale):
-    scores = jnp.einsum("nqhd,nkhd->nhqk", queries, keys_all, preferred_element_type=jnp.float32)
-    return scores * score_scale
+def dot_plain(first_side, second_side):
+    return jnp.dot(first_side, second_side, preferred_element_type=jnp.float32)
+
+
+def key_weights(queries, keys_all):
+    scores = dot_last(keys_all, queries) * DH ** (-0.5)
+    key_ids = lax.broadcasted_iota(jnp.int32, scores.shape, 0)
+    scores = jnp.where(key_ids < SEQ, scores, -1e30)
+    powers = jnp.exp(scores - jnp.max(scores, axis=0, keepdims=True))
+    return powers * (1.0 / jnp.sum(powers, axis=0, keepdims=True))
+
+
+def forward_kernel(rows_ref, qkv_weight, out_weight, qkv_ref, context_ref, parts_ref, padded):
+    images = rows_ref.shape[0]
+    span = padded.shape[0]
+    heads = qkv_weight.shape[1] // (3 * DH)
+
+    def one_image(image, unused):
+        padded[...] = jnp.zeros_like(padded)
+        padded[0:SEQ, :] = rows_ref[image]
+        qkv_ref[image] = dot_plain(padded[...], qkv_weight[...]).astype(jnp.bfloat16)
+        for pair in range(heads // 2):
+            block = qkv_ref[image, :, 6 * DH * pair : 6 * DH * (pair + 1)]
+            found = []
+            for head in range(2):
+                base = 3 * DH * head
+                weights = key_weights(
+                    block[:, base : base + DH], block[:, base + DH : base + 2 * DH]
+                ).astype(jnp.bfloat16)
+                found.append(dot_rows(weights, block[:, base + 2 * DH : base + 3 * DH]))
+            context_ref[image, :, 2 * DH * pair : 2 * DH * (pair + 1)] = jnp.concatenate(
+                found, axis=1
+            ).astype(jnp.bfloat16)
+        parts_ref[image] = dot_plain(context_ref[image], out_weight[...])[0:SEQ]
+        return unused
+
+    lax.fori_loop(0, images, one_image, 0)
+
+
+def attention_forward(rows, qkv_weight, out_weight):
+    images, unused, model_width = rows.shape
+    span = -(-SEQ // 128) * 128
+    in_vmem = pl.BlockSpec(memory_space=pltpu.VMEM)
+    return pl.pallas_call(
+        forward_kernel,
+        out_shape=(
+            jax.ShapeDtypeStruct((images, span, qkv_weight.shape[1]), jnp.bfloat16),
+            jax.ShapeDtypeStruct((images, span, out_weight.shape[0]), jnp.bfloat16),
+            jax.ShapeDtypeStruct((images, SEQ, model_width), jnp.float32),
+        ),
+        in_specs=[in_vmem] * 3,
+        out_specs=(in_vmem,) * 3,
+        scratch_shapes=[pltpu.VMEM((span, model_width), jnp.bfloat16)],
+        name="attention_forward",
+    )(rows, qkv_weight, out_weight)
+
+
+def backward_kernel(
+    rows_ref,
+    grad_ref,
+    qkv_ref,
+    context_ref,
+    qkv_weight,
+    out_weight,
+    qkv_grad,
+    out_grad,
+    normed_grad,
+    rows_padded,
+    grad_padded,
+    grad_context,
+    grad_qkv,
+):
+    images, span = qkv_ref.shape[0], qkv_ref.shape[1]
+    heads = qkv_weight.shape[1] // (3 * DH)
+    scale = DH ** (-0.5)
+    rows_padded[...] = jnp.zeros_like(rows_padded)
+    grad_padded[...] = jnp.zeros_like(grad_padded)
+
+    def one_image(image, unused):
+        rows_padded[image, 0:SEQ, :] = rows_ref[image]
+        grad_padded[image, 0:SEQ, :] = grad_ref[image]
+        grad_context[...] = dot_last(grad_padded[image], out_weight[...]).astype(jnp.bfloat16)
+        for pair in range(heads // 2):
+            block = qkv_ref[image, :, 6 * DH * pair : 6 * DH * (pair + 1)]
+            grads = grad_context[:, 2 * DH * pair : 2 * DH * (pair + 1)]
+            found = []
+            for head in range(2):
+                base = 3 * DH * head
+                queries = block[:, base : base + DH]
+                keys_all = block[:, base + DH : base + 2 * DH]
+                values_all = block[:, base + 2 * DH : base + 3 * DH]
+                head_grad = grads[:, DH * head : DH * (head + 1)]
+                weights = key_weights(queries, keys_all)
+                grad_values = dot_plain(weights.astype(jnp.bfloat16), head_grad)
+                grad_weights = dot_last(values_all, head_grad)
+                row_term = jnp.sum(grad_weights * weights, axis=0, keepdims=True)
+                grad_scores = (weights * (grad_weights - row_term)).astype(jnp.bfloat16)
+                grad_queries = dot_rows(grad_scores, keys_all) * scale
+                grad_keys = dot_plain(grad_scores, queries) * scale
+                found += [grad_queries, grad_keys, grad_values]
+            grad_qkv[image, :, 6 * DH * pair : 6 * DH * (pair + 1)] = jnp.concatenate(
+                found, axis=1
+            ).astype(jnp.bfloat16)
+        normed_grad[image] = dot_last(grad_qkv[image], qkv_weight[...])[0:SEQ].astype(jnp.bfloat16)
+        return unused
+
+    lax.fori_loop(0, images, one_image, 0)
+
+    def flat(ref):
+        return ref[...].reshape(images * span, ref.shape[2])
+
+    qkv_grad[...] = dot_rows(flat(rows_padded), flat(grad_qkv)).astype(jnp.bfloat16)
+    out_grad[...] = dot_rows(flat(context_ref), flat(grad_padded)).astype(jnp.bfloat16)
+
+
+def attention_backward(rows, grad_rows, qkv, context, qkv_weight, out_weight):
+    images, unused, model_width = rows.shape
+    span = qkv.shape[1]
+    in_vmem = pl.BlockSpec(memory_space=pltpu.VMEM)
+    return pl.pallas_call(
+        backward_kernel,
+        out_shape=(
+            jax.ShapeDtypeStruct(qkv_weight.shape, jnp.bfloat16),
+            jax.ShapeDtypeStruct(out_weight.shape, jnp.bfloat16),
+            jax.ShapeDtypeStruct((images, SEQ, model_width), jnp.bfloat16),
+        ),
+        in_specs=[in_vmem] * 6,
+        out_specs=(in_vmem,) * 3,
+        scratch_shapes=[
+            pltpu.VMEM((images, span, model_width), jnp.bfloat16),
+            pltpu.VMEM((images, span, model_width), jnp.bfloat16),
+            pltpu.VMEM((span, out_weight.shape[0]), jnp.bfloat16),
+            pltpu.VMEM((images, span, qkv_weight.shape[1]), jnp.bfloat16),
+        ],
+        name="attention_backward",
+    )(rows, grad_rows, qkv, context, qkv_weight, out_weight)
 
 
 def share_over_cores(parts, col_place):
-    theirs = lax.dynamic_index_in_dim(parts, 1 - col_place, 0, keepdims=False)
-    ours = lax.dynamic_index_in_dim(parts, col_place, 0, keepdims=False)
+    count = parts.shape[0] // 2
+    theirs = lax.dynamic_slice_in_dim(parts, (1 - col_place) * count, count, 0)
+    ours = lax.dynamic_slice_in_dim(parts, col_place * count, count, 0)
+    theirs = theirs.reshape(count * SEQ, -1)
+    ours = ours.reshape(count * SEQ, -1)
     return ours, lax.ppermute(theirs, "cols", [(0, 1), (1, 0)])
 
 
@@ -248,8 +388,6 @@
     model_width = tokens_in.shape[1]
     experts = router_weight.shape[1]
     capacity = max(2, 8 * local_rows // (3 * experts))
-    heads_local = qkv_weight.shape[1] // (3 * DH)
-    score_scale = DH ** (-0.5)
     row_place = lax.axis_index("rows")
     col_place = lax.axis_index("cols")
     device_count = lax.axis_size("rows") * lax.axis_size("cols")
@@ -286,26 +424,9 @@
     cotangent_arrived = to_experts(cotangent)
     tokens_f = tokens_in.astype(jnp.float32)
     normed_low = layer_norm(tokens_f, ln1_gain, ln1_shift).astype(jnp.bfloat16)
-    gathered = lax.all_gather(normed_low, "cols", axis=0, tiled=True)
-    pair_rows = gathered.shape[0]
-    images = pair_rows // SEQ
-    qkv_low = jnp.dot(gathered, qkv_weight, preferred_element_type=jnp.float32).astype(jnp.bfloat16)
-    head_split = qkv_low.reshape(images, SEQ, heads_local, 3, DH)
-    queries = head_split[:, :, :, 0]
-    keys_all = head_split[:, :, :, 1]
-    values_all = head_split[:, :, :, 2]
-    scores = attention_scores(queries, keys_all, score_scale)
-    score_peak = jnp.max(scores, axis=-1, keepdims=True)
-    log_total = score_peak + jnp.log(jnp.sum(jnp.exp(scores - score_peak), axis=-1, keepdims=True))
-    weights_low = jnp.exp(scores - log_total).astype(jnp.bfloat16)
-    context = jnp.einsum(
-        "nhqk,nkhd->nqhd", weights_low, values_all, preferred_element_type=jnp.float32
-    )
-    context_low = context.astype(jnp.bfloat16).reshape(pair_rows, heads_local * DH)
-    attn_parts = jnp.dot(context_low, out_weight, preferred_element_type=jnp.float32)
-    attn_ours, attn_theirs = share_over_cores(
-        attn_parts.reshape(images, SEQ, model_width), col_place
-    )
+    gathered = lax.all_gather(normed_low.reshape(-1, SEQ, model_width), "cols", axis=0, tiled=True)
+    qkv_low, context_low, attn_parts = attention_forward(gathered, qkv_weight, out_weight)
+    attn_ours, attn_theirs = share_over_cores(attn_parts, col_place)
     attn_out = attn_ours + attn_theirs
     hidden_one = tokens_f + attn_out
     mixed_low = layer_norm(hidden_one, ln2_gain, ln2_shift).astype(jnp.bfloat16)
@@ -315,7 +436,8 @@
     chosen = (routes[:, :, None] == expert_ids[None, None, :]).astype(jnp.float32)
     gate_values = jnp.sum(router_probs[:, None, :] * chosen, axis=-1)
     grad_out = cotangent.astype(jnp.float32)
-    arrived = to_experts(mixed_low)
+    mixed_sent, cotangent_arrived = lax.optimization_barrier((mixed_low, cotangent_arrived))
+    arrived = to_experts(mixed_sent)
     own_expert = (row_place * lax.axis_size("cols") + col_place) // copies
     arrived_probs = jax.nn.softmax(
         jnp.dot(arrived, router_weight, preferred_element_type=jnp.float32), axis=-1
@@ -334,6 +456,9 @@
     grad_pre_low = (grad_act * gelu_slope(pre_act)).astype(jnp.bfloat16)
     grad_arrived = dot_last(grad_pre_low, expert_in).astype(jnp.bfloat16)
     grad_sent = swap_slots(grad_arrived)
+    arrived, grad_pre_low, act_low, grad_result, unused_rows = lax.optimization_barrier(
+        (arrived, grad_pre_low, act_low, grad_result, grad_arrived)
+    )
     first_grad = dot_rows(arrived, grad_pre_low)
     second_grad = dot_rows(act_low, grad_result)
     picked_one = jnp.dot(place_one, returned, preferred_element_type=jnp.float32)
@@ -354,42 +479,13 @@
     grad_hidden_part, ln2_gain_grad, ln2_shift_grad = norm_two_back(grad_mixed)
     grad_hidden = grad_out + grad_hidden_part
     grad_attn_low = grad_hidden.astype(jnp.bfloat16)
-    grad_attn_all = lax.all_gather(grad_attn_low, "cols", axis=0, tiled=True)
-    out_grad = dot_rows(context_low, grad_attn_all)
-    grad_context = (
-        dot_last(grad_attn_all, out_weight)
-        .astype(jnp.bfloat16)
-        .reshape(images, SEQ, heads_local, DH)
-    )
-    scores_again = attention_scores(queries, keys_all, score_scale)
-    attn_probs = jnp.exp(scores_again - log_total)
-    probs_low = attn_probs.astype(jnp.bfloat16)
-    grad_values = jnp.einsum(
-        "nhqk,nqhd->nkhd", probs_low, grad_context, preferred_element_type=jnp.float32
-    )
-    grad_weights = jnp.einsum(
-        "nqhd,nkhd->nhqk", grad_context, values_all, preferred_element_type=jnp.float32
-    )
-    row_term = jnp.sum(grad_weights * attn_probs, axis=-1, keepdims=True)
-    grad_scores = (attn_probs * (grad_weights - row_term)).astype(jnp.bfloat16)
-    grad_queries = (
-        jnp.einsum("nhqk,nkhd->nqhd", grad_scores, keys_all, preferred_element_type=jnp.float32)
-        * score_scale
-    )
-    grad_keys = (
-        jnp.einsum("nhqk,nqhd->nkhd", grad_scores, queries, preferred_element_type=jnp.float32)
-        * score_scale
-    )
-    grad_qkv = (
-        jnp.stack([grad_queries, grad_keys, grad_values], axis=3)
-        .astype(jnp.bfloat16)
-        .reshape(pair_rows, 3 * heads_local * DH)
-    )
-    qkv_grad = dot_rows(gathered, grad_qkv)
-    normed_ours, normed_theirs = share_over_cores(
-        dot_last(grad_qkv, qkv_weight).astype(jnp.bfloat16).reshape(images, SEQ, model_width),
-        col_place,
-    )
+    grad_attn_all = lax.all_gather(
+        grad_attn_low.reshape(-1, SEQ, model_width), "cols", axis=0, tiled=True
+    )
+    qkv_grad, out_grad, normed_parts = attention_backward(
+        gathered, grad_attn_all, qkv_low, context_low, qkv_weight, out_weight
+    )
+    normed_ours, normed_theirs = share_over_cores(normed_parts, col_place)
     grad_normed = normed_ours.astype(jnp.float32) + normed_theirs.astype(jnp.float32)
     unused_one, norm_one_back = jax.vjp(layer_norm, tokens_f, ln1_gain, ln1_shift)
     grad_tokens_part, ln1_gain_grad, ln1_shift_grad = norm_one_back(grad_normed)
@@ -406,7 +502,7 @@
         axis=0,
     )
     qkv_grad, out_grad, small_sum = sum_over_devices(
-        qkv_grad.astype(jnp.bfloat16), out_grad.astype(jnp.bfloat16), small_part
+        qkv_grad, out_grad, small_part
     )
     router_grad = small_sum[:experts].T
     ln1_gain_grad, ln1_shift_grad, ln2_gain_grad, ln2_shift_grad = (

time: 268 us -> 248 us (0.925)
  local copies, waits for them, and re-layouts: 41.5 us -> 6.65 us
  waiting for transfers between devices: 25.1 us -> 58.2 us
  matrix products: 79.8 us -> 59.2 us
  Pallas kernels: 68.8 us -> 80.9 us
  starting transfers between devices: 23.4 us -> 18.8 us
  other arithmetic: 21.6 us -> 17.3 us
    all_to_all x4, waiting for transfers between devices: 23.9 us -> 58.2 us  [swap_slots(): lax.all_to_all(slot_rows.reshape(device_count, capacity, model_width), ('...]
    pallas_call x0 -> x2, Pallas kernels: none -> 19.4 us  [the longest x1 12.9 us: attention_backward(): pl.pallas_call(backward_kernel, out_shape=(jax.ShapeDtypeStruct(qkv_weigh...]
    unnamed x95 -> x44, local copies, waits for them, and re-layouts: 15.8 us -> 0.13 us
    dot_general x8 -> x0, matrix products: 10.6 us -> none  [the longest x1 2.41 us: body(): jnp.einsum('nhqk,nqhd->nkhd', probs_low, grad_context, preferred_element_...]
    pallas_call x1, Pallas kernels: 68.8 us -> 61.6 us  [sum_over_devices(): pl.pallas_call(sum_kernel, out_shape=(jax.ShapeDtypeStruct(qkv_shape, jnp...]
    slice x1 -> x0, local copies, waits for them, and re-layouts: 6.89 us -> none  [body(): queries = head_split[:, :, :, 0]]
    reshape x5 -> x2, local copies, waits for them, and re-layouts: 8.92 us -> 2.1 us  [share_over_cores(): theirs = theirs.reshape(count * SEQ, -1)]
    all_to_all x4, starting transfers between devices: 22.7 us -> 18.1 us  [swap_slots(): lax.all_to_all(slot_rows.reshape(device_count, capacity, model_width), ('...]
  transfers between devices with their start and end apart: 6 -> 6, of which waited for: 3 -> 4; matrix products, arithmetic and copies ran while one was open for 26% -> 14% of each run, Pallas kernels for 0% -> 0%
where the time goes in v2:
time: 248 us; the launch traced here: 247 us
  Pallas kernels  80.9 us (33%)
  matrix products  59.2 us (24%)
  waiting for transfers between devices  58.2 us (23%)
  starting transfers between devices  18.8 us (8%)
  other arithmetic  17.3 us (7%)
  local copies, waits for them, and re-layouts  6.65 us (3%)
  blocking collectives  5.06 us (2%)
    pallas_call x1, Pallas kernels, sum_over_devices(): pl.pallas_call(sum_kernel, out_shape=(jax.ShapeDtypeStruct(qkv_shape, jnp...  61.6 us
    all_to_all x4, waiting for transfers between devices, swap_slots(): lax.all_to_all(slot_rows.reshape(device_count, capacity, model_width), ('...  58.2 us
    all_to_all x4, starting transfers between devices, swap_slots(): lax.all_to_all(slot_rows.reshape(device_count, capacity, model_width), ('...  18.1 us
    dot_general x1, matrix products, body(): pre_act = jnp.dot(arrived, expert_in, preferred_element_type=jnp.float32)  17.8 us
    dot_general x5, matrix products, dot_rows(): lax.dot_general(first_side, second_side, (((0,), (0,)), ((), ())), prefer...  16.8 us
    dot_general x3, matrix products, dot_last(): lax.dot_general(first_side, second_side, (((1,), (1,)), ((), ())), prefer...  13.1 us
    pallas_call x1, Pallas kernels, attention_backward(): pl.pallas_call(backward_kernel, out_shape=(jax.ShapeDtypeStruct(qkv_weigh...  12.9 us
    dot_general x1, matrix products, body(): jnp.dot(act_low, expert_out, preferred_element_type=jnp.float32)  6.99 us
  transfers between devices with their start and end apart: 6, of which 4 were waited for; matrix products, arithmetic and copies ran while one was open for 14% of the time, Pallas kernels for 0%

profile of v2, /device:TPU:0, one launch (start us, length us, event | category | flops | bytes accessed | tf_op | source)
XLA Modules:
  0.0 247.2 jit_solution(1193484591762601483)
XLA Ops:
  1.9 1.2 fusion.25
  3.1 1.2 fusion.32
  4.3 2.5 all-gather.2.rows_ref
  6.8 6.5 %attention_forward.1 = (bf16[2,256,1152]{2,1,0:T(8,128)(2,1)}, bf16[2,256,384]{2,1,0:T(8,128)(2,1)}, f32[2,197,768]{2,1,0:T(8,128)}) custom-call(bf16[2,197,768]{2,1,0:T(8,128)(2,1)} %all-gather.2.rows_ref, bf16[768,1152]{1,0:T(8,128)(2,1)} %qkv_weight.3, bf16[384,768]{1,0:T(8,128)(2,1)} %out_weight.3), custom_call_target="tpu_custom_call" | custom-call | tf_op jit(solution)/shard_map/attention_forward/pallas_call | solution.py:269
  15.2 1.5 convolution_convert_fusion.3
  16.7 7.0 %all-to-all-start = ((bf16[32,16,768]{2,1,0:T(8,128)(2,1)}), bf16[32,16,768]{2,1,0:T(8,128)(2,1)S(1)}, u32[]{:S(2)}, u32[]{:S(2)}) async-start(bf16[32,16,768]{2,1,0:T(8,128)(2,1)} %bitcast.6), calls=%async_computation | async-start | bytes 1572864 | tf_op jit(solution)/shard_map/all_to_all | solution.py:415
  23.7 1.3 fusion.63
  25.5 18.8 %all-to-all-done = bf16[32,16,768]{2,1,0:T(8,128)(2,1)S(1)} async-done(((bf16[32,16,768]{2,1,0:T(8,128)(2,1)}), bf16[32,16,768]{2,1,0:T(8,128)(2,1)S(1)}, u32[]{:S(2)}, u32[]{:S(2)}) %all-to-all-start) | async-done | bytes 786464 | tf_op jit(solution)/shard_map/all_to_all | solution.py:415
  44.3 1.5 convolution_convert_fusion.2
  45.8 3.6 %all-to-all-start.1 = ((bf16[32,16,768]{2,1,0:T(8,128)(2,1)}), bf16[32,16,768]{2,1,0:T(8,128)(2,1)S(1)}, u32[]{:S(2)}, u32[]{:S(2)}) async-start(bf16[32,16,768]{2,1,0:T(8,128)(2,1)} %bitcast.80), calls=%async_computation.1 | async-start | bytes 1572864 | tf_op jit(solution)/shard_map/all_to_all | solution.py:415
  49.8 20.3 %all-to-all-done.1 = bf16[32,16,768]{2,1,0:T(8,128)(2,1)S(1)} async-done(((bf16[32,16,768]{2,1,0:T(8,128)(2,1)}), bf16[32,16,768]{2,1,0:T(8,128)(2,1)S(1)}, u32[]{:S(2)}, u32[]{:S(2)}) %all-to-all-start.1) | async-done | bytes 786464 | tf_op jit(solution)/shard_map/all_to_all | solution.py:415
  70.4 17.8 %fusion.2 = (bf16[512,3072]{1,0:T(8,128)(2,1)S(1)}, f32[512,3072]{1,0:T(8,128)}) fusion(bf16[512,768]{1,0:T(8,128)(2,1)S(1)} %bitcast.73, bf16[768,3072]{1,0:T(8,128)(2,1)} %param.20), kind=kOutput, calls=%fused_computation.4 | convolution fusion | flops 2518155264 | bytes 14942208 | tf_op jit(solution)/shard_map/dot_general | solution.py:449
  88.2 7.0 %convolution_convert_fusion.1 = bf16[512,768]{1,0:T(8,128)(2,1)} fusion(bf16[512,3072]{1,0:T(8,128)(2,1)S(1)} %get-tuple-element.39, bf16[3072,768]{1,0:T(8,128)(2,1)} %param.21), kind=kOutput, calls=%fused_computation.29 | convolution fusion | flops 2416312320 | bytes 8650752 | tf_op jit(solution)/shard_map/dot_general | solution.py:451
  95.2 3.8 %all-to-all-start.2 = ((bf16[32,16,768]{2,1,0:T(8,128)(2,1)}), bf16[32,16,768]{2,1,0:T(8,128)(2,1)S(1)}, u32[]{:S(2)}, u32[]{:S(2)}) async-start(bf16[32,16,768]{2,1,0:T(8,128)(2,1)} %bitcast.81), calls=%async_computation.2 | async-start | bytes 1572864 | tf_op jit(solution)/shard_map/all_to_all | solution.py:415
  99.3 7.0 %fusion.8 = bf16[512,3072]{1,0:T(8,128)(2,1)S(1)} fusion(f32[512,3072]{1,0:T(8,128)} %get-tuple-element.67, bf16[512,768]{1,0:T(8,128)(2,1)S(1)} %multiply_convert_fusion, bf16[3072,768]{1,0:T(8,128)(2,1)} %param.21), kind=kOutput, calls=%fused_computation.10 | convolution fusion | flops 2431647744 | bytes 14942208 | tf_op jit(solution)/shard_map/dot_general | solution.py:36
  106.3 5.9 %convolution_convert_fusion = bf16[512,768]{1,0:T(8,128)(2,1)} fusion(bf16[512,3072]{1,0:T(8,128)(2,1)S(1)} %fusion.8, bf16[768,3072]{1,0:T(8,128)(2,1)} %param.20), kind=kOutput, calls=%fused_computation.28 | convolution fusion | flops 2416312320 | bytes 8650752 | tf_op jit(solution)/shard_map/dot_general | solution.py:36
  112.1 5.2 %fusion.70 = f32[768,3072]{1,0:T(8,128)} fusion(bf16[512,768]{1,0:T(8,128)(2,1)S(1)} %bitcast.74, bf16[512,3072]{1,0:T(8,128)(2,1)S(1)} %fusion.8), kind=kOutput, calls=%fused_computation.135 | convolution fusion | flops 2415919104 | bytes 13369344 | tf_op jit(solution)/shard_map/dot_general | solution.py:30
  117.3 2.1 all-to-all-done.2
  119.4 3.7 %all-to-all-start.3 = ((bf16[32,16,768]{2,1,0:T(8,128)(2,1)}), bf16[32,16,768]{2,1,0:T(8,128)(2,1)}, u32[]{:S(2)}, u32[]{:S(2)}) async-start(bf16[32,16,768]{2,1,0:T(8,128)(2,1)} %bitcast.79), calls=%async_computation.3 | async-start | bytes 1572864 | tf_op jit(solution)/shard_map/all_to_all | solution.py:415
  123.6 1.4 fusion.27
  126.7 17.0 %all-to-all-done.3 = bf16[32,16,768]{2,1,0:T(8,128)(2,1)} async-done(((bf16[32,16,768]{2,1,0:T(8,128)(2,1)}), bf16[32,16,768]{2,1,0:T(8,128)(2,1)}, u32[]{:S(2)}, u32[]{:S(2)}) %all-to-all-start.3) | async-done | bytes 786464 | tf_op jit(solution)/shard_map/all_to_all | solution.py:415
  143.8 1.8 multiply_reduce_fusion
  146.2 1.8 fusion.62
  148.2 2.6 %all-gather.3.grad_ref = bf16[2,197,768]{2,1,0:T(8,128)(2,1)} all-gather(bf16[1,197,768]{2,1,0:T(8,128)(2,1)S(1)} %fusion.31), channel_id=3, replica_groups=mesh['rows'=16,'cols'=2] {'cols'}, dimensions={0}, use_global_device_ids=true | all-gather | bytes 907776 | tf_op jit(solution)/shard_map/all_gather | solution.py:482
  150.8 12.9 %attention_backward.1 = (bf16[768,1152]{1,0:T(8,128)(2,1)}, bf16[384,768]{1,0:T(8,128)(2,1)}, bf16[2,197,768]{2,1,0:T(8,128)(2,1)}) custom-call(bf16[2,197,768]{2,1,0:T(8,128)(2,1)} %all-gather.2.rows_ref, bf16[2,197,768]{2,1,0:T(8,128)(2,1)} %all-gather.3.grad_ref, bf16[2,256,1152]{2,1,0:T(8,128)(2,1)} %get-tuple-element.29.qkv_ref, ...), custom_call_target="tpu_custom_call" | custom-call | tf_op jit(solution)/shard_map/attention_backward/pallas_call | solution.py:345
  165.0 8.5 %fusion.71 = f32[3072,768]{1,0:T(8,128)} fusion(bf16[512,3072]{1,0:T(8,128)(2,1)} %copy-done.21, bf16[512,768]{1,0:T(8,128)(2,1)} %copy-done.7), kind=kOutput, calls=%fused_computation.136 | convolution fusion | flops 2415919104 | bytes 13369344 | tf_op jit(solution)/shard_map/dot_general | solution.py:30
  174.5 1.3 concatenate.3.small_ref
  175.8 61.6 %sum_gradients.1 = (bf16[16,48,1152]{2,1,0:T(8,128)(2,1)}, bf16[16,24,768]{2,1,0:T(8,128)(2,1)}, f32[40,768]{1,0:T(8,128)}) custom-call(bf16[16,48,1152]{2,1,0:T(8,128)(2,1)} %bitcast.78, bf16[16,24,768]{2,1,0:T(8,128)(2,1)} %bitcast.82, f32[40,768]{1,0:T(8,128)} %concatenate.3.small_ref), custom_call_target="tpu_custom_call" | custom-call | tf_op jit(solution)/shard_map/sum_gradients/pallas_call | solution.py:195
  237.4 1.6 slice_reduce_fusion
  238.9 1.5 slice_bitcast_fusion
  240.5 2.2 bitcast_convert_fusion.1
  242.6 3.5 %bitcast_convert_fusion = f32[768,1152]{1,0:T(8,128)} fusion(bf16[16,48,1152]{2,1,0:T(8,128)(2,1)} %get-tuple-element.35), kind=kLoop, calls=%fused_computation.26 | loop fusion | flops 884736 | bytes 5308416 | tf_op jit(solution)/shard_map/reshape | solution.py:220
  (89 shorter events, 10.7 us)
Async XLA Ops:
  0.6 48.8 %copy-start = (bf16[768,32]{0,1:T(8,128)(2,1)S(1)}, bf16[768,32]{0,1:T(8,128)(2,1)}, u32[]{:S(2)}) copy-start(bf16[768,32]{0,1:T(8,128)(2,1)} %param.19) | copy-start | bytes 147460
  0.7 23.0 %copy-start.1 = (bf16[197,768]{1,0:T(8,128)(2,1)S(1)}, bf16[197,768]{1,0:T(8,128)(2,1)}, u32[]{:S(2)}) copy-start(bf16[197,768]{1,0:T(8,128)(2,1)} %param.12) | copy-start | bytes 907780
  0.7 14.1 %copy-start.17 = (s32[197,2]{0,1:T(2,128)S(1)}, s32[197,2]{0,1:T(2,128)}, u32[]{:S(2)}) copy-start(s32[197,2]{0,1:T(2,128)} %param.22) | copy-start | bytes 4732
  0.7 14.5 %copy-start.4 = (bf16[197,768]{1,0:T(8,128)(2,1)S(1)}, bf16[197,768]{1,0:T(8,128)(2,1)}, u32[]{:S(2)}) copy-start(bf16[197,768]{1,0:T(8,128)(2,1)} %param.23) | copy-start | bytes 907780
  3.1 11.3 %copy-start.14 = (f32[197]{0:T(256)}, f32[197]{0:T(256)S(1)}, u32[]{:S(2)}) copy-start(f32[197]{0:T(256)S(1)} %fusion.25) | copy-start | bytes 2368
  3.1 22.2 %copy-start.11 = (f32[768]{0:T(1024)S(1)}, f32[768]{0:T(1024)}, u32[]{:S(2)}) copy-start(f32[768]{0:T(1024)} %param.17) | copy-start | bytes 9220
  3.1 22.2 %copy-start.18 = (f32[768]{0:T(1024)S(1)}, f32[768]{0:T(1024)}, u32[]{:S(2)}) copy-start(f32[768]{0:T(1024)} %param.18) | copy-start | bytes 9220
  14.4 9.3 %collective-permute-start = (f32[197,768]{1,0:T(8,128)S(1)}, f32[197,768]{1,0:T(8,128)S(1)}, u32[]{:S(2)}, u32[]{:S(2)}) collective-permute-start(f32[197,768]{1,0:T(8,128)S(1)} %dynamic-slice_bitcast_fusion), channel_id=1, source_target_pairs={{0,1},{1,0},{2,3},{3,2},{4,5},{5,4},{6,7},{7,6},{8,9},{9,8},{10,11... | collective-permute-start | bytes 1815560 | tf_op jit(solution)/shard_map/ppermute | solution.py:370
  14.8 55.2 %copy-start.19 = (s32[197,1]{0,1:T(1,128)}, s32[197,1]{0,1:T(1,128)S(1)}, u32[]{:S(2)}) copy-start(s32[197,1]{0,1:T(1,128)S(1)} %get-tuple-element.62) | copy-start | bytes 2368
  14.8 108.3 %copy-start.20 = (s32[197,1]{0,1:T(1,128)}, s32[197,1]{0,1:T(1,128)S(1)}, u32[]{:S(2)}) copy-start(s32[197,1]{0,1:T(1,128)S(1)} %get-tuple-element.63) | copy-start | bytes 2368
  15.2 73.0 %copy-start.8 = (pred[197,512]{1,0:T(8,128)(4,1)}, pred[197,512]{1,0:T(8,128)(4,1)S(1)}, u32[]{:S(2)}) copy-start(pred[197,512]{1,0:T(8,128)(4,1)S(1)} %convolution_compare_fusion) | copy-start | bytes 302596
  16.7 27.6 %all-to-all-start = ((bf16[32,16,768]{2,1,0:T(8,128)(2,1)}), bf16[32,16,768]{2,1,0:T(8,128)(2,1)S(1)}, u32[]{:S(2)}, u32[]{:S(2)}) async-start(bf16[32,16,768]{2,1,0:T(8,128)(2,1)} %bitcast.6), calls=%async_computation | async-start | bytes 1572864 | tf_op jit(solution)/shard_map/all_to_all | solution.py:415
  25.2 44.8 %copy-start.16 = (f32[197]{0:T(256)}, f32[197]{0:T(256)S(1)}, u32[]{:S(2)}) copy-start(f32[197]{0:T(256)S(1)} %multiply_reduce_fusion.2) | copy-start | bytes 2368
  25.3 24.2 %copy-start.13 = (f32[197]{0:T(256)}, f32[197]{0:T(256)S(1)}, u32[]{:S(2)}) copy-start(f32[197]{0:T(256)S(1)} %fusion.57) | copy-start | bytes 2368
  25.4 62.7 %copy-start.2 = (bf16[197,768]{1,0:T(8,128)(2,1)}, bf16[197,768]{1,0:T(8,128)(2,1)S(1)}, u32[]{:S(2)}) copy-start(bf16[197,768]{1,0:T(8,128)(2,1)S(1)} %add_convert_fusion.2) | copy-start | bytes 907780
  45.8 24.2 %all-to-all-start.1 = ((bf16[32,16,768]{2,1,0:T(8,128)(2,1)}), bf16[32,16,768]{2,1,0:T(8,128)(2,1)S(1)}, u32[]{:S(2)}, u32[]{:S(2)}) async-start(bf16[32,16,768]{2,1,0:T(8,128)(2,1)} %bitcast.80), calls=%async_computation.1 | async-start | bytes 1572864 | tf_op jit(solution)/shard_map/all_to_all | solution.py:415
  49.7 38.5 %copy-start.12 = (f32[197]{0:T(256)}, f32[197]{0:T(256)S(1)}, u32[]{:S(2)}) copy-start(f32[197]{0:T(256)S(1)} %fusion.47) | copy-start | bytes 2368
  88.2 7.0 %copy-start.21 = (bf16[512,3072]{1,0:T(8,128)(2,1)}, bf16[512,3072]{1,0:T(8,128)(2,1)S(1)}, u32[]{:S(2)}) copy-start(bf16[512,3072]{1,0:T(8,128)(2,1)S(1)} %get-tuple-element.39) | copy-start | bytes 9437188
  95.2 24.2 %all-to-all-start.2 = ((bf16[32,16,768]{2,1,0:T(8,128)(2,1)}), bf16[32,16,768]{2,1,0:T(8,128)(2,1)S(1)}, u32[]{:S(2)}, u32[]{:S(2)}) async-start(bf16[32,16,768]{2,1,0:T(8,128)(2,1)} %bitcast.81), calls=%async_computation.2 | async-start | bytes 1572864 | tf_op jit(solution)/shard_map/all_to_all | solution.py:415
  99.3 12.8 %copy-start.7 = (bf16[512,768]{1,0:T(8,128)(2,1)}, bf16[512,768]{1,0:T(8,128)(2,1)S(1)}, u32[]{:S(2)}) copy-start(bf16[512,768]{1,0:T(8,128)(2,1)S(1)} %multiply_convert_fusion) | copy-start | bytes 2359300
  112.1 11.0 %copy-start.9 = (pred[197,512]{1,0:T(8,128)(4,1)S(1)}, pred[197,512]{1,0:T(8,128)(4,1)}, u32[]{:S(2)}) copy-start(pred[197,512]{1,0:T(8,128)(4,1)} %copy-done.8) | copy-start | bytes 302596
  112.1 11.4 %copy-start.5 = (bf16[197,768]{1,0:T(8,128)(2,1)S(1)}, bf16[197,768]{1,0:T(8,128)(2,1)}, u32[]{:S(2)}) copy-start(bf16[197,768]{1,0:T(8,128)(2,1)} %param.23) | copy-start | bytes 907780
  119.4 24.4 %all-to-all-start.3 = ((bf16[32,16,768]{2,1,0:T(8,128)(2,1)}), bf16[32,16,768]{2,1,0:T(8,128)(2,1)}, u32[]{:S(2)}, u32[]{:S(2)}) async-start(bf16[32,16,768]{2,1,0:T(8,128)(2,1)} %bitcast.79), calls=%async_computation.3 | async-start | bytes 1572864 | tf_op jit(solution)/shard_map/all_to_all | solution.py:415
  164.8 8.8 %copy-start.3 = (bf16[197,768]{1,0:T(8,128)(2,1)S(1)}, bf16[197,768]{1,0:T(8,128)(2,1)}, u32[]{:S(2)}) copy-start(bf16[197,768]{1,0:T(8,128)(2,1)} %copy-done.2) | copy-start | bytes 907780
  164.8 9.0 %copy-start.6 = (bf16[2,197,768]{2,1,0:T(8,128)(2,1)S(1)}, bf16[2,197,768]{2,1,0:T(8,128)(2,1)}, u32[]{:S(2)}) copy-start(bf16[2,197,768]{2,1,0:T(8,128)(2,1)} %get-tuple-element.31) | copy-start | bytes 1815556
  164.8 9.0 %copy-start.10 = (f32[768]{0:T(1024)S(1)}, f32[768]{0:T(1024)}, u32[]{:S(2)}) copy-start(f32[768]{0:T(1024)} %param.13) | copy-start | bytes 9220
  164.8 9.2 %copy-start.15 = (f32[197]{0:T(256)S(1)}, f32[197]{0:T(256)}, u32[]{:S(2)}) copy-start(f32[197]{0:T(256)} %copy-done.14) | copy-start | bytes 2368
  164.8 8.9 %collective-permute-start.1 = (bf16[197,768]{1,0:T(8,128)(2,1)S(1)}, bf16[197,768]{1,0:T(8,128)(2,1)S(1)}, u32[]{:S(2)}, u32[]{:S(2)}) collective-permute-start(bf16[197,768]{1,0:T(8,128)(2,1)S(1)} %dynamic-slice_bitcast_fusion.1), channel_id=1, source_target_pairs={{0,1},{1,0},{2,3},{3,2},{4,5},{5,4},{6,7},{7,6},{8,9},{9,8},{10,11... | collective-permute-start | bytes 907784 | tf_op jit(solution)/shard_map/ppermute | solution.py:370

commit v3 on v2

--- a/solution.py
+++ b/solution.py
@@ -413,15 +413,14 @@
 
     def swap_slots(slot_rows):
         swapped = lax.all_to_all(
-            slot_rows.reshape(device_count, capacity, model_width),
+            slot_rows.reshape(device_count, capacity, slot_rows.shape[1]),
             ("rows", "cols"),
             split_axis=0,
             concat_axis=0,
             tiled=True,
         )
-        return swapped.reshape(device_count * capacity, model_width)
-
-    cotangent_arrived = to_experts(cotangent)
+        return swapped.reshape(slot_rows.shape)
+
     tokens_f = tokens_in.astype(jnp.float32)
     normed_low = layer_norm(tokens_f, ln1_gain, ln1_shift).astype(jnp.bfloat16)
     gathered = lax.all_gather(normed_low.reshape(-1, SEQ, model_width), "cols", axis=0, tiled=True)
@@ -436,8 +435,9 @@
     chosen = (routes[:, :, None] == expert_ids[None, None, :]).astype(jnp.float32)
     gate_values = jnp.sum(router_probs[:, None, :] * chosen, axis=-1)
     grad_out = cotangent.astype(jnp.float32)
-    mixed_sent, cotangent_arrived = lax.optimization_barrier((mixed_low, cotangent_arrived))
-    arrived = to_experts(mixed_sent)
+    arrived = to_experts(mixed_low)
+    cotangent_sent, unused_rows = lax.optimization_barrier((cotangent, mixed_low))
+    cotangent_arrived = to_experts(cotangent_sent)
     own_expert = (row_place * lax.axis_size("cols") + col_place) // copies
     arrived_probs = jax.nn.softmax(
         jnp.dot(arrived, router_weight, preferred_element_type=jnp.float32), axis=-1
@@ -451,25 +451,47 @@
     result_low = jnp.dot(act_low, expert_out, preferred_element_type=jnp.float32).astype(
         jnp.bfloat16
     )
-    returned = swap_slots(result_low)
+    gate_slots = jnp.sum(
+        cotangent_arrived.astype(jnp.float32) * result_low.astype(jnp.float32),
+        axis=-1,
+        keepdims=True,
+    )
+    gate_high = lax.reduce_precision(gate_slots, 8, 7)
+    gate_middle = lax.reduce_precision(gate_slots - gate_high, 8, 7)
+    gate_low = gate_slots - gate_high - gate_middle
+    lanes = jnp.arange(128, dtype=jnp.int32)[None, :]
+    gate_lanes = jnp.where(
+        lanes == 0,
+        gate_high,
+        jnp.where(lanes == 1, gate_middle, jnp.where(lanes == 2, gate_low, 0.0)),
+    ).astype(jnp.bfloat16)
     grad_act = dot_last(grad_result, expert_out)
     grad_pre_low = (grad_act * gelu_slope(pre_act)).astype(jnp.bfloat16)
     grad_arrived = dot_last(grad_pre_low, expert_in).astype(jnp.bfloat16)
-    grad_sent = swap_slots(grad_arrived)
+    grad_sent = swap_slots(jnp.concatenate([grad_arrived, gate_lanes], axis=1))
     arrived, grad_pre_low, act_low, grad_result, unused_rows = lax.optimization_barrier(
         (arrived, grad_pre_low, act_low, grad_result, grad_arrived)
     )
     first_grad = dot_rows(arrived, grad_pre_low)
     second_grad = dot_rows(act_low, grad_result)
+    gates_sent = grad_sent[:, model_width:]
+    grad_gates = jnp.stack(
+        [
+            jnp.sum(jnp.dot(place, gates_sent, preferred_element_type=jnp.float32), axis=-1)
+            for place in (place_one, place_two)
+        ],
+        axis=1,
+    )
+    grad_mixed_experts = jnp.dot(
+        place_any, grad_sent[:, :model_width], preferred_element_type=jnp.float32
+    )
+    result_sent, unused_sent = lax.optimization_barrier((result_low, grad_sent))
+    returned = swap_slots(result_sent)
     picked_one = jnp.dot(place_one, returned, preferred_element_type=jnp.float32)
     picked_two = jnp.dot(place_two, returned, preferred_element_type=jnp.float32)
     output = (
         hidden_one + gate_values[:, 0:1] * picked_one + gate_values[:, 1:2] * picked_two
     ).astype(jnp.bfloat16)
-    grad_gates = jnp.stack(
-        [jnp.sum(grad_out * picked_one, axis=-1), jnp.sum(grad_out * picked_two, axis=-1)], axis=1
-    )
-    grad_mixed_experts = jnp.dot(place_any, grad_sent, preferred_element_type=jnp.float32)
     gate_term = jnp.sum(grad_gates * gate_values, axis=-1, keepdims=True)
     grad_probs = jnp.sum(chosen * grad_gates[:, :, None], axis=1)
     grad_logits_low = (router_probs * (grad_probs - gate_term)).astype(jnp.bfloat16)

time: 248 us -> 225 us (0.907)
  waiting for transfers between devices: 58.2 us -> 32.7 us
  Pallas kernels: 80.9 us -> 86.3 us
  matrix products: 59.2 us -> 53.9 us
    all_to_all x4, waiting for transfers between devices: 58.2 us -> 31.5 us  [swap_slots(): lax.all_to_all(slot_rows.reshape(device_count, capacity, slot_rows.shape[...]
    pallas_call x1, Pallas kernels: 61.6 us -> 66.8 us  [sum_over_devices(): pl.pallas_call(sum_kernel, out_shape=(jax.ShapeDtypeStruct(qkv_shape, jnp...]
    dot_general x3, matrix products: 13.1 us -> 8.86 us  [dot_last(): lax.dot_general(first_side, second_side, (((1,), (1,)), ((), ())), prefer...]
  transfers between devices with their start and end apart: 6 -> 6, of which waited for: 4 -> 4; matrix products, arithmetic and copies ran while one was open for 14% -> 22% of each run, Pallas kernels for 0% -> 30%
where the time goes in v3:
time: 225 us; the launch traced here: 224 us
  Pallas kernels  86.3 us (38%)
  matrix products  53.9 us (24%)
  waiting for transfers between devices  32.7 us (15%)
  starting transfers between devices  19.5 us (9%)
  other arithmetic  17.6 us (8%)
  local copies, waits for them, and re-layouts  7.87 us (3%)
  blocking collectives  4.84 us (2%)
    pallas_call x1, Pallas kernels, sum_over_devices(): pl.pallas_call(sum_kernel, out_shape=(jax.ShapeDtypeStruct(qkv_shape, jnp...  66.8 us
    all_to_all x4, waiting for transfers between devices, swap_slots(): lax.all_to_all(slot_rows.reshape(device_count, capacity, slot_rows.shape[...  31.5 us
    all_to_all x4, starting transfers between devices, swap_slots(): lax.all_to_all(slot_rows.reshape(device_count, capacity, slot_rows.shape[...  18.9 us
    dot_general x1, matrix products, body(): pre_act = jnp.dot(arrived, expert_in, preferred_element_type=jnp.float32)  18.1 us
    dot_general x5, matrix products, dot_rows(): lax.dot_general(first_side, second_side, (((0,), (0,)), ((), ())), prefer...  15.5 us
    pallas_call x1, Pallas kernels, attention_backward(): pl.pallas_call(backward_kernel, out_shape=(jax.ShapeDtypeStruct(qkv_weigh...  12.9 us
    dot_general x3, matrix products, dot_last(): lax.dot_general(first_side, second_side, (((1,), (1,)), ((), ())), prefer...  8.86 us
    dot_general x1, matrix products, body(): jnp.dot(act_low, expert_out, preferred_element_type=jnp.float32)  6.98 us
  transfers between devices with their start and end apart: 6, of which 4 were waited for; matrix products, arithmetic and copies ran while one was open for 22% of the time, Pallas kernels for 30%

profile of v3, /device:TPU:0, one launch (start us, length us, event | category | flops | bytes accessed | tf_op | source)
XLA Modules:
  0.0 223.9 jit_solution(10177160727842809110)
XLA Ops:
  4.3 2.5 %all-gather.2.rows_ref = bf16[2,197,768]{2,1,0:T(8,128)(2,1)} all-gather(bf16[1,197,768]{2,1,0:T(8,128)(2,1)S(1)} %fusion.36), channel_id=2, replica_groups=mesh['rows'=16,'cols'=2] {'cols'}, dimensions={0}, use_global_device_ids=true | all-gather | bytes 907776 | tf_op jit(solution)/shard_map/all_gather | solution.py:426
  6.7 6.5 %attention_forward.1 = (bf16[2,256,1152]{2,1,0:T(8,128)(2,1)}, bf16[2,256,384]{2,1,0:T(8,128)(2,1)}, f32[2,197,768]{2,1,0:T(8,128)}) custom-call(bf16[2,197,768]{2,1,0:T(8,128)(2,1)} %all-gather.2.rows_ref, bf16[768,1152]{1,0:T(8,128)(2,1)} %qkv_weight.3, bf16[384,768]{1,0:T(8,128)(2,1)} %out_weight.3), custom_call_target="tpu_custom_call" | custom-call | tf_op jit(solution)/shard_map/attention_forward/pallas_call | solution.py:269
  15.2 1.3 collective-permute-done
  16.5 1.2 fusion.57
  18.1 1.5 convolution_convert_fusion.3
  19.6 7.2 %all-to-all-start = ((bf16[32,16,768]{2,1,0:T(8,128)(2,1)}), bf16[32,16,768]{2,1,0:T(8,128)(2,1)S(1)}, u32[]{:S(2)}, u32[]{:S(2)}) async-start(bf16[32,16,768]{2,1,0:T(8,128)(2,1)} %bitcast.6), calls=%async_computation | async-start | bytes 1572864 | tf_op jit(solution)/shard_map/all_to_all | solution.py:415
  26.9 1.5 convolution_convert_fusion.1
  28.4 19.1 %all-to-all-done = bf16[32,16,768]{2,1,0:T(8,128)(2,1)S(1)} async-done(((bf16[32,16,768]{2,1,0:T(8,128)(2,1)}), bf16[32,16,768]{2,1,0:T(8,128)(2,1)S(1)}, u32[]{:S(2)}, u32[]{:S(2)}) %all-to-all-start) | async-done | bytes 786464 | tf_op jit(solution)/shard_map/all_to_all | solution.py:415
  47.5 3.8 %all-to-all-start.1 = ((bf16[32,16,768]{2,1,0:T(8,128)(2,1)}), bf16[32,16,768]{2,1,0:T(8,128)(2,1)S(1)}, u32[]{:S(2)}, u32[]{:S(2)}) async-start(bf16[32,16,768]{2,1,0:T(8,128)(2,1)} %bitcast.84), calls=%async_computation.1 | async-start | bytes 1572864 | tf_op jit(solution)/shard_map/all_to_all | solution.py:415
  51.3 18.1 %fusion.2 = (bf16[512,3072]{1,0:T(8,128)(2,1)}, f32[512,3072]{1,0:T(8,128)}) fusion(bf16[512,768]{1,0:T(8,128)(2,1)S(1)} %bitcast.74, bf16[768,3072]{1,0:T(8,128)(2,1)} %param.20), kind=kOutput, calls=%fused_computation.4 | convolution fusion | flops 2518155264 | bytes 14942208 | tf_op jit(solution)/shard_map/dot_general | solution.py:449
  69.8 1.9 all-to-all-done.1
  71.7 7.0 %fusion.16 = (bf16[512,768]{1,0:T(8,128)(2,1)S(1)}, f32[512]{0:T(512)S(1)}, bf16[512,768]{1,0:T(8,128)(2,1)}) fusion(bf16[32,16,768]{2,1,0:T(8,128)(2,1)S(1)} %all-to-all-done.1, f32[512]{0:T(512)S(1)} %select_reduce_fusion.1, bf16[512,3072]{1,0:T(8,128)(2,1)} %get-tuple-element.39, bf16[3072,768]{1,0:T(8,128)(2,1)} %param.21), kind=kOutput, calls=%fused_computation.29 | convolution fusion | flops 2418671104 | bytes 10227712 | tf_op jit(solution)/shard_map/dot_general | solution.py:451
  78.7 6.0 %fusion.8 = bf16[512,3072]{1,0:T(8,128)(2,1)S(1)} fusion(f32[512,3072]{1,0:T(8,128)S(1)} %copy-done.18, bf16[512,768]{1,0:T(8,128)(2,1)S(1)} %get-tuple-element.40, bf16[3072,768]{1,0:T(8,128)(2,1)} %param.21), kind=kOutput, calls=%fused_computation.10 | convolution fusion | flops 2431647744 | bytes 14942208 | tf_op jit(solution)/shard_map/dot_general | solution.py:36
  84.7 2.6 %convolution_convert_fusion = bf16[512,768]{1,0:T(8,128)(2,1)S(1)} fusion(bf16[512,3072]{1,0:T(8,128)(2,1)S(1)} %fusion.8, bf16[768,3072]{1,0:T(8,128)(2,1)S(1)} %bitcast.105), kind=kOutput, calls=%fused_computation.31 | convolution fusion | flops 2416312320 | bytes 8650752 | tf_op jit(solution)/shard_map/dot_general | solution.py:36
  88.7 4.0 %all-to-all-start.2 = ((bf16[32,16,896]{2,1,0:T(8,128)(2,1)}), bf16[32,16,896]{2,1,0:T(8,128)(2,1)S(1)}, u32[]{:S(2)}, u32[]{:S(2)}) async-start(bf16[32,16,896]{2,1,0:T(8,128)(2,1)} %bitcast.11), calls=%async_computation.2 | async-start | bytes 1835008 | tf_op jit(solution)/shard_map/all_to_all | solution.py:415
  93.0 7.2 %fusion.65 = f32[768,3072]{1,0:T(8,128)} fusion(bf16[512,768]{1,0:T(8,128)(2,1)S(1)} %bitcast.76, bf16[512,3072]{1,0:T(8,128)(2,1)} %copy-done.2), kind=kOutput, calls=%fused_computation.143 | convolution fusion | flops 2415919104 | bytes 13369344 | tf_op jit(solution)/shard_map/dot_general | solution.py:30
  100.3 5.2 %fusion.66 = f32[3072,768]{1,0:T(8,128)} fusion(bf16[512,3072]{1,0:T(8,128)(2,1)S(1)} %copy-done.15, bf16[512,768]{1,0:T(8,128)(2,1)S(1)} %copy-done.17), kind=kOutput, calls=%fused_computation.144 | convolution fusion | flops 2415919104 | bytes 13369344 | tf_op jit(solution)/shard_map/dot_general | solution.py:30
  105.5 10.5 %all-to-all-done.2 = bf16[32,16,896]{2,1,0:T(8,128)(2,1)S(1)} async-done(((bf16[32,16,896]{2,1,0:T(8,128)(2,1)}), bf16[32,16,896]{2,1,0:T(8,128)(2,1)S(1)}, u32[]{:S(2)}, u32[]{:S(2)}) %all-to-all-start.2) | async-done | bytes 917536 | tf_op jit(solution)/shard_map/all_to_all | solution.py:415
  117.0 1.3 multiply_reduce_fusion
  118.8 2.4 %all-gather.3.grad_ref = bf16[2,197,768]{2,1,0:T(8,128)(2,1)} all-gather(bf16[1,197,768]{2,1,0:T(8,128)(2,1)S(1)} %fusion.35), channel_id=3, replica_groups=mesh['rows'=16,'cols'=2] {'cols'}, dimensions={0}, use_global_device_ids=true | all-gather | bytes 907776 | tf_op jit(solution)/shard_map/all_gather | solution.py:504
  121.2 12.9 %attention_backward.1 = (bf16[768,1152]{1,0:T(8,128)(2,1)}, bf16[384,768]{1,0:T(8,128)(2,1)}, bf16[2,197,768]{2,1,0:T(8,128)(2,1)}) custom-call(bf16[2,197,768]{2,1,0:T(8,128)(2,1)} %all-gather.2.rows_ref, bf16[2,197,768]{2,1,0:T(8,128)(2,1)} %all-gather.3.grad_ref, bf16[2,256,1152]{2,1,0:T(8,128)(2,1)} %get-tuple-element.29.qkv_ref, ...), custom_call_target="tpu_custom_call" | custom-call | tf_op jit(solution)/shard_map/attention_backward/pallas_call | solution.py:345
  134.1 1.7 dynamic-slice_bitcast_fusion.1
  136.6 3.9 %all-to-all-start.3 = ((bf16[32,16,768]{2,1,0:T(8,128)(2,1)}), bf16[32,16,768]{2,1,0:T(8,128)(2,1)S(1)}, u32[]{:S(2)}, u32[]{:S(2)}) async-start(bf16[32,16,768]{2,1,0:T(8,128)(2,1)} %bitcast.83), calls=%async_computation.3 | async-start | bytes 1572864 | tf_op jit(solution)/shard_map/all_to_all | solution.py:415
  140.7 1.3 fusion.32
  141.9 1.4 fusion.30
  143.4 1.3 concatenate.7.small_ref
  144.7 66.8 %sum_gradients.1 = (bf16[16,48,1152]{2,1,0:T(8,128)(2,1)}, bf16[16,24,768]{2,1,0:T(8,128)(2,1)}, f32[40,768]{1,0:T(8,128)}) custom-call(bf16[16,48,1152]{2,1,0:T(8,128)(2,1)} %bitcast.79, bf16[16,24,768]{2,1,0:T(8,128)(2,1)} %bitcast.85, f32[40,768]{1,0:T(8,128)} %concatenate.7.small_ref), custom_call_target="tpu_custom_call" | custom-call | tf_op jit(solution)/shard_map/sum_gradients/pallas_call | solution.py:195
  211.5 1.5 slice_reduce_fusion
  213.1 1.5 slice_bitcast_fusion
  214.6 2.2 bitcast_convert_fusion.1
  216.8 2.1 add_convert_fusion
  218.8 3.5 %bitcast_convert_fusion = f32[768,1152]{1,0:T(8,128)} fusion(bf16[16,48,1152]{2,1,0:T(8,128)(2,1)} %get-tuple-element.35), kind=kLoop, calls=%fused_computation.28 | loop fusion | flops 884736 | bytes 5308416 | tf_op jit(solution)/shard_map/reshape | solution.py:220
  (95 shorter events, 12.0 us)
Async XLA Ops:
  0.6 68.7 %copy-start = (bf16[768,32]{0,1:T(8,128)(2,1)S(1)}, bf16[768,32]{0,1:T(8,128)(2,1)}, u32[]{:S(2)}) copy-start(bf16[768,32]{0,1:T(8,128)(2,1)} %param.19) | copy-start | bytes 147460
  0.7 15.8 %copy-start.1 = (bf16[197,768]{1,0:T(8,128)(2,1)S(1)}, bf16[197,768]{1,0:T(8,128)(2,1)}, u32[]{:S(2)}) copy-start(bf16[197,768]{1,0:T(8,128)(2,1)} %param.12) | copy-start | bytes 907780
  0.7 14.1 %copy-start.7 = (s32[197,2]{0,1:T(2,128)S(1)}, s32[197,2]{0,1:T(2,128)}, u32[]{:S(2)}) copy-start(s32[197,2]{0,1:T(2,128)} %param.22) | copy-start | bytes 4732
  0.7 17.3 %copy-start.5 = (f32[768]{0:T(1024)S(1)}, f32[768]{0:T(1024)}, u32[]{:S(2)}) copy-start(f32[768]{0:T(1024)} %param.17) | copy-start | bytes 9220
  0.7 17.3 %copy-start.8 = (f32[768]{0:T(1024)S(1)}, f32[768]{0:T(1024)}, u32[]{:S(2)}) copy-start(f32[768]{0:T(1024)} %param.18) | copy-start | bytes 9220
  6.7 20.1 %copy-start.3 = (bf16[197,768]{1,0:T(8,128)(2,1)S(1)}, bf16[197,768]{1,0:T(8,128)(2,1)}, u32[]{:S(2)}) copy-start(bf16[197,768]{1,0:T(8,128)(2,1)} %param.23) | copy-start | bytes 907780
  14.3 2.1 collective-permute-start
  14.8 101.1 %copy-start.12 = (s32[197,1]{0,1:T(1,128)}, s32[197,1]{0,1:T(1,128)S(1)}, u32[]{:S(2)}) copy-start(s32[197,1]{0,1:T(1,128)S(1)} %get-tuple-element.65) | copy-start | bytes 2368
  14.8 101.5 %copy-start.9 = (s32[197,1]{0,1:T(1,128)}, s32[197,1]{0,1:T(1,128)S(1)}, u32[]{:S(2)}) copy-start(s32[197,1]{0,1:T(1,128)S(1)} %get-tuple-element.64) | copy-start | bytes 2368
  19.6 27.8 %all-to-all-start = ((bf16[32,16,768]{2,1,0:T(8,128)(2,1)}), bf16[32,16,768]{2,1,0:T(8,128)(2,1)S(1)}, u32[]{:S(2)}, u32[]{:S(2)}) async-start(bf16[32,16,768]{2,1,0:T(8,128)(2,1)} %bitcast.6), calls=%async_computation | async-start | bytes 1572864 | tf_op jit(solution)/shard_map/all_to_all | solution.py:415
  47.5 24.2 %all-to-all-start.1 = ((bf16[32,16,768]{2,1,0:T(8,128)(2,1)}), bf16[32,16,768]{2,1,0:T(8,128)(2,1)S(1)}, u32[]{:S(2)}, u32[]{:S(2)}) async-start(bf16[32,16,768]{2,1,0:T(8,128)(2,1)} %bitcast.84), calls=%async_computation.1 | async-start | bytes 1572864 | tf_op jit(solution)/shard_map/all_to_all | solution.py:415
  71.7 7.0 %copy-start.18 = (f32[512,3072]{1,0:T(8,128)S(1)}, f32[512,3072]{1,0:T(8,128)}, u32[]{:S(2)}) copy-start(f32[512,3072]{1,0:T(8,128)} %get-tuple-element.67) | copy-start | bytes 18874372
  71.7 13.0 %slice-start = ((s8[4718592]{0:T(1024)(128)(4,1)}), s8[4194304]{0:T(1024)(128)(4,1)S(1)}, s32[]{:S(2)}) async-start(s8[4718592]{0:T(1024)(128)(4,1)} %bitcast.104), calls=%async_computation.4 | async-start | bytes 8388608
  78.7 6.0 %copy-start.16 = (bf16[512,768]{1,0:T(8,128)(2,1)}, bf16[512,768]{1,0:T(8,128)(2,1)S(1)}, u32[]{:S(2)}) copy-start(bf16[512,768]{1,0:T(8,128)(2,1)S(1)} %get-tuple-element.40) | copy-start | bytes 2359300
  78.7 6.0 %slice-start.1 = ((s8[4718592]{0:T(1024)(128)(4,1)}), s8[524288]{0:T(1024)(128)(4,1)S(1)}, s32[]{:S(2)}) async-start(s8[4718592]{0:T(1024)(128)(4,1)} %bitcast.104), calls=%async_computation.5 | async-start | bytes 1048576
  84.7 2.7 %copy-start.2 = (bf16[512,3072]{1,0:T(8,128)(2,1)}, bf16[512,3072]{1,0:T(8,128)(2,1)S(1)}, u32[]{:S(2)}) copy-start(bf16[512,3072]{1,0:T(8,128)(2,1)S(1)} %fusion.8) | copy-start | bytes 9437188
  88.7 27.2 %all-to-all-start.2 = ((bf16[32,16,896]{2,1,0:T(8,128)(2,1)}), bf16[32,16,896]{2,1,0:T(8,128)(2,1)S(1)}, u32[]{:S(2)}, u32[]{:S(2)}) async-start(bf16[32,16,896]{2,1,0:T(8,128)(2,1)} %bitcast.11), calls=%async_computation.2 | async-start | bytes 1835008 | tf_op jit(solution)/shard_map/all_to_all | solution.py:415
  93.0 7.2 %copy-start.15 = (bf16[512,3072]{1,0:T(8,128)(2,1)S(1)}, bf16[512,3072]{1,0:T(8,128)(2,1)}, u32[]{:S(2)}) copy-start(bf16[512,3072]{1,0:T(8,128)(2,1)} %get-tuple-element.39) | copy-start | bytes 9437188
  93.0 7.2 %copy-start.17 = (bf16[512,768]{1,0:T(8,128)(2,1)S(1)}, bf16[512,768]{1,0:T(8,128)(2,1)}, u32[]{:S(2)}) copy-start(bf16[512,768]{1,0:T(8,128)(2,1)} %copy-done.16) | copy-start | bytes 2359300
  118.3 22.3 %copy-start.4 = (f32[768]{0:T(1024)S(1)}, f32[768]{0:T(1024)}, u32[]{:S(2)}) copy-start(f32[768]{0:T(1024)} %param.13) | copy-start | bytes 9220
  118.7 24.7 %copy-start.6 = (f32[197]{0:T(256)}, f32[197]{0:T(256)S(1)}, u32[]{:S(2)}) copy-start(f32[197]{0:T(256)S(1)} %negate_multiply_fusion.2) | copy-start | bytes 2368
  135.8 4.8 %collective-permute-start.1 = (bf16[197,768]{1,0:T(8,128)(2,1)}, bf16[197,768]{1,0:T(8,128)(2,1)S(1)}, u32[]{:S(2)}, u32[]{:S(2)}) collective-permute-start(bf16[197,768]{1,0:T(8,128)(2,1)} %dynamic-slice_bitcast_fusion.1), channel_id=1, source_target_pairs={{0,1},{1,0},{2,3},{3,2},{4,5},{5,4},{6,7},{7,6},{8,9},{9,8},{10,11... | collective-permute-start | bytes 907784 | tf_op jit(solution)/shard_map/ppermute | solution.py:370
  136.6 85.8 %all-to-all-start.3 = ((bf16[32,16,768]{2,1,0:T(8,128)(2,1)}), bf16[32,16,768]{2,1,0:T(8,128)(2,1)S(1)}, u32[]{:S(2)}, u32[]{:S(2)}) async-start(bf16[32,16,768]{2,1,0:T(8,128)(2,1)} %bitcast.83), calls=%async_computation.3 | async-start | bytes 1572864 | tf_op jit(solution)/shard_map/all_to_all | solution.py:415
  143.3 79.0 %copy-start.13 = (s32[197,1]{0,1:T(1,128)S(1)}, s32[197,1]{0,1:T(1,128)}, u32[]{:S(2)}) copy-start(s32[197,1]{0,1:T(1,128)} %copy-done.12) | copy-start | bytes 2368
  143.3 79.0 %copy-start.14 = (f32[197,1]{0,1:T(1,128)S(1)}, f32[197,1]{0,1:T(1,128)}, u32[]{:S(2)}) copy-start(f32[197,1]{0,1:T(1,128)} %get-tuple-element.60) | copy-start | bytes 2368
  144.7 78.0 %copy-start.10 = (s32[197,1]{0,1:T(1,128)S(1)}, s32[197,1]{0,1:T(1,128)}, u32[]{:S(2)}) copy-start(s32[197,1]{0,1:T(1,128)} %copy-done.9) | copy-start | bytes 2368
  144.7 78.0 %copy-start.11 = (f32[197,1]{0,1:T(1,128)S(1)}, f32[197,1]{0,1:T(1,128)}, u32[]{:S(2)}) copy-start(f32[197,1]{0,1:T(1,128)} %get-tuple-element.59) | copy-start | bytes 2368
